TPU v7x, 32 devices: a whole 2x2x4 slice. The times are simulated.
32 devices in a mesh: wide: 8 (over z, x), narrow: 4 (over y, core).
Axes of the slice: x: 2, y: 2, z: 4, core: 2. Of those that a mesh axis runs over, the one named last changes fastest.
Arguments:
- star_pos: float32 [3, 2048], P(None, ('wide', 'narrow')), may hold values from -6 to 6
- star_vel: float32 [3, 2048], P(None, ('wide', 'narrow')), may hold values from -6 to 6
- star_mass: float32 [2048], P(('wide', 'narrow')), may hold values from 0.00048828125 to 0.0048828125
- star_acc: float32 [3, 2048], P(None, ('wide', 'narrow')), may hold values from -6 to 6
- star_jerk: float32 [3, 2048], P(None, ('wide', 'narrow')), may hold values from -120 to 120
- gal_pos: float32 [3, 16384], P(None, ('wide', 'narrow')), may hold values from -6 to 6
- gal_vel: float32 [3, 16384], P(None, ('wide', 'narrow')), may hold values from -6 to 6
- gal_mass: float32 [16384], P(('wide', 'narrow')), may hold values from 0.0009765625 to 0.009765625
- group_of: int32 [16384], P(('wide', 'narrow')), may hold values from 0 to 31, as said below
- let_send: int32 [32, 8, 1], P(('wide', 'narrow')), may hold values from -1 to 3, as said below
- star_leaf: int32 [128, 8], P(('wide', 'narrow')), may hold values from 0 to 7, as said below
Outputs:
- gal_vel_new: float32 [3, 16384], P(None, ('wide', 'narrow'))
- star_pos_new: float32 [3, 2048], P(None, ('wide', 'narrow'))
- star_vel_new: float32 [3, 2048], P(None, ('wide', 'narrow'))
Inputs may be any that keep to these rules, and one draw needn't show every extreme that they name: `group_of`: within each leaf of 128 bodies every group number is held by exactly 4 bodies. `let_send`: entry [k, j, s] is a local leaf of device k sent to the device of wide index j with k's narrow index, or -1 for an empty slot; the leaves of one row are distinct; a device lists nothing for its own wide index; for some wide index j, every device whose wide index is not j lists a leaf for j, in every draw. `star_leaf`: the star blocks listed for one leaf are distinct.
All inputs are finite; a program needn't handle non-finite values.
Results may differ from a plain program's by a relative error of at most 0.0003.
Values sent between devices are 32-bit elements; how exact they have to be, the bound alone decides.
A program may use at most 64 MiB of HBM per device.

v0:
```python
import functools

import jax
import jax.numpy as jnp
from jax import lax
from jax.experimental import pallas as pl
from jax.experimental.pallas import tpu as pltpu
from jax.sharding import PartitionSpec as P

GROUPS = 32
LANES = 128
ROWS = 8
BODY_UNROLL = 32
STAR_UNROLL = 16
MESH = pl.DeviceIdType.MESH

time_step = 0.25
soften_sq = 0.05


def loop(count, step, init, most=4):
    unroll = next(u for u in range(min(most, count), 0, -1) if count % u == 0)
    return lax.fori_loop(0, count, step, init, unroll=unroll)


def spread(row):
    return jnp.broadcast_to(row, (ROWS, row.shape[1]))


def column(block, index):
    return jnp.broadcast_to(block[:, index : index + 1], (ROWS, LANES))


def pull(source, mass, target, total):
    dx, dy, dz = (s - t for s, t in zip(source, target))
    inverse = lax.rsqrt(dx * dx + dy * dy + dz * dz + soften_sq)
    weight = mass * inverse * inverse * inverse
    return (total[0] + dx * weight, total[1] + dy * weight, total[2] + dz * weight)


def kernel(
    n_wide,
    n_narrow,
    star_pos_hbm,
    star_vel_hbm,
    star_mass_hbm,
    star_acc_hbm,
    star_jerk_hbm,
    gal_pos_hbm,
    gal_vel_hbm,
    gal_mass_hbm,
    group_of_hbm,
    let_send_hbm,
    star_leaf_hbm,
    out,
    star_pos,
    star_vel,
    star_mass,
    star_acc,
    star_jerk,
    gal_pos,
    gal_vel,
    gal_mass,
    group_of,
    let_send,
    star_leaf,
    in_sem,
    states,
    cell_out,
    cell_in,
    cols,
    srow,
    crow,
    send_sem,
    recv_sem,
    cell_send_sem,
    cell_recv_sem,
    pass_send_sem,
    pass_recv_sem,
):
    wide, narrow = lax.axis_index("wide"), lax.axis_index("narrow")
    stars = star_pos.shape[1]
    bodies = gal_pos.shape[1]
    leaves, kicks = star_leaf.shape
    slots = LANES // GROUPS
    step_sq = time_step * time_step

    fetches = [
        pltpu.make_async_copy(source, target, in_sem.at[i])
        for i, (source, target) in enumerate(
            (
                (star_pos_hbm, star_pos),
                (star_vel_hbm, star_vel),
                (star_mass_hbm, star_mass),
                (star_acc_hbm, star_acc),
                (star_jerk_hbm, star_jerk),
                (gal_pos_hbm, gal_pos),
                (gal_vel_hbm, gal_vel),
                (gal_mass_hbm, gal_mass),
                (group_of_hbm, group_of),
                (let_send_hbm, let_send),
                (star_leaf_hbm, star_leaf),
            )
        )
    ]
    barrier = pltpu.get_barrier_semaphore()

    def greet(w, n):
        pl.semaphore_signal(barrier, inc=1, device_id=(w, n), device_id_type=MESH)

    beside = [narrow] + [lax.rem(narrow + m, n_narrow) for m in range(1, n_narrow)]

    def each_wide(first, step):
        lax.fori_loop(first, n_wide, step, 0, unroll=n_wide <= 16)

    def greet_peers(j, carry):
        w = lax.rem(wide + j, n_wide)
        for n in beside:
            greet(w, n)
        return carry

    each_wide(1, greet_peers)
    for n in beside[1:]:
        greet(wide, n)

    for fetch in fetches:
        fetch.start()

    lane = lax.broadcasted_iota(jnp.int32, (1, LANES), 1)
    lane4 = lax.broadcasted_iota(jnp.int32, (4, LANES), 1)
    lane8 = lax.broadcasted_iota(jnp.int32, (ROWS, LANES), 1)
    row8 = lax.broadcasted_iota(jnp.int32, (ROWS, LANES), 0)
    left = lane4 < stars

    for fetch in fetches:
        fetch.wait()

    spos, svel = star_pos[...], star_vel[...]
    sacc, sjerk = star_acc[...], star_jerk[...]
    pred_pos = (
        spos + time_step * svel + step_sq * 0.5 * sacc + step_sq * time_step / 6.0 * sjerk
    )
    pred_vel = svel + time_step * sacc + step_sq * 0.5 * sjerk
    pos4 = jnp.concatenate([pred_pos, star_mass[...]], axis=0)
    vel4 = jnp.concatenate([pred_vel, jnp.zeros((1, stars), jnp.float32)], axis=0)
    block = jnp.concatenate([pos4, vel4], axis=1)
    block = jnp.where(lax.rem(wide, 2) == 0, block, pltpu.roll(block, stars, 1))
    states[narrow, wide] = block
    both = jnp.concatenate([pos4, vel4], axis=0)
    targets = jnp.transpose(
        jnp.concatenate([both, jnp.zeros((ROWS, LANES - stars), jnp.float32)], axis=1)
    )

    gpos, gmass = gal_pos[...], gal_mass[...]
    body_lane = lax.broadcasted_iota(jnp.int32, (1, bodies), 1)
    segment = group_of[...] + (body_lane // (bodies // leaves)) * GROUPS
    onehot = (
        lax.broadcasted_iota(jnp.int32, (LANES, bodies), 0)
        == jnp.broadcast_to(segment, (LANES, bodies))
    ).astype(jnp.float32)
    moments = jnp.concatenate(
        [gpos * gmass, gmass, jnp.zeros((4, bodies), jnp.float32)], axis=0
    )
    sums = lax.dot_general(
        moments,
        onehot,
        (((1,), (1,)), ((), ())),
        precision=lax.Precision.HIGHEST,
        preferred_element_type=jnp.float32,
    )
    cells = jnp.where(row8 < 3, sums / spread(sums[3:4]), sums)
    crow[0] = cells

    group = lane // GROUPS
    part = jnp.bitwise_and(group - lax.rem(wide, slots), slots - 1)
    square = (n_wide, n_wide)
    diagonal = lax.broadcasted_iota(jnp.int32, square, 0) == lax.broadcasted_iota(
        jnp.int32, square, 1
    )
    listed = jnp.broadcast_to(let_send[...].astype(jnp.float32), square)
    chosen = jnp.sum(jnp.where(diagonal, listed, 0.0), axis=1, keepdims=True)
    chosen = jnp.broadcast_to(chosen, (n_wide, LANES)).astype(jnp.int32)
    outgoing = jnp.zeros((n_wide, LANES), jnp.float32)
    pick = jnp.bitwise_and(group - chosen, slots - 1)
    for k in range(slots):
        turned = cells if k == 0 else pltpu.roll(cells, k * GROUPS, 1)
        base = jnp.zeros((1, LANES), jnp.float32)
        for c in range(4):
            base = jnp.where(part == c, turned[c : c + 1], base)
        outgoing = jnp.where(
            jnp.logical_and(pick == k, chosen >= 0),
            jnp.broadcast_to(base, (n_wide, LANES)),
            outgoing,
        )
    cell_out[:, 0, :] = outgoing
    cell_in[wide] = jnp.zeros((1, LANES), jnp.float32)

    pl.semaphore_wait(barrier, n_wide * n_narrow - 1)

    def send_state(w, n, sends, recvs):
        pltpu.make_async_remote_copy(
            src_ref=states.at[narrow, wide],
            dst_ref=states.at[narrow, wide],
            send_sem=sends,
            recv_sem=recvs,
            device_id=(w, n),
            device_id_type=MESH,
        ).start()

    def send_wide(j, carry):
        w = lax.rem(wide + j, n_wide)
        pltpu.make_async_remote_copy(
            src_ref=cell_out.at[w],
            dst_ref=cell_in.at[wide],
            send_sem=cell_send_sem,
            recv_sem=cell_recv_sem,
            device_id=(w, narrow),
            device_id_type=MESH,
        ).start()
        send_state(w, narrow, send_sem, recv_sem)
        return carry

    def send_others(j, carry):
        w = lax.rem(wide + j, n_wide)
        for n in beside[1:]:
            send_state(w, n, pass_send_sem, pass_recv_sem)
        return carry

    each_wide(1, send_wide)
    each_wide(1, send_others)
    for n in beside[1:]:
        send_state(wide, n, pass_send_sem, pass_recv_sem)

    tiles = bodies // LANES
    body_rows = jnp.concatenate(
        [gpos, gmass, jnp.zeros((4, bodies), jnp.float32)], axis=0
    )
    for t in range(tiles):
        cols[t * LANES : (t + 1) * LANES, :] = jnp.transpose(
            body_rows[:, t * LANES : (t + 1) * LANES]
        )
    here = [
        [spread(gpos[c : c + 1, t * LANES : (t + 1) * LANES]) for c in range(3)]
        for t in range(tiles)
    ]

    def on_bodies(start, which, total):
        source = cols[pl.ds(pl.multiple_of(start, ROWS), ROWS), :]
        place = [column(source, c) for c in range(3)]
        mass = column(source, 3)
        return tuple(pull(place, mass, here[t], total[i]) for i, t in enumerate(which))

    every = tuple(range(tiles))
    zero = jnp.zeros((ROWS, LANES), jnp.float32)
    total = tuple((zero, zero, zero) for _ in every)
    total = loop(bodies // ROWS, lambda g, acc: on_bodies(g * ROWS, every, acc), total, BODY_UNROLL)

    some = states.at[0, pl.ds(0, n_wide - 1)]
    pltpu.make_async_copy(some, some, recv_sem).wait()
    few = cell_in.at[pl.ds(0, n_wide - 1)]
    pltpu.make_async_copy(few, few, cell_recv_sem).wait()
    halves = n_wide // 2

    def star_rows(n, i):
        even_block, odd_block = states[n, 2 * i], states[n, 2 * i + 1]
        rows = jnp.where(left, even_block, odd_block)
        spot = n * halves + i
        srow[spot, 0:4, :] = rows
        srow[spot, 4:8, :] = pltpu.roll(jnp.where(left, odd_block, even_block), stars, 1)
        return rows

    def star_cols(i, carry):
        rows = jnp.concatenate(
            [star_rows(narrow, i), jnp.zeros((4, LANES), jnp.float32)], axis=0
        )
        start = pl.multiple_of(bodies + i * LANES, LANES)
        cols[pl.ds(start, LANES), :] = jnp.transpose(rows)
        return carry

    loop(halves, star_cols, 0)
    ess_start = bodies + n_wide * stars

    def ess_rows(e, carry):
        parts = []
        for c in range(4):
            row = jnp.zeros((1, LANES), jnp.float32)
            for k in range(slots):
                row = jnp.where(group == (c + k) % slots, cell_in[e * slots + k], row)
            parts.append(row if c == 0 else pltpu.roll(row, LANES - c * GROUPS, 1))
        parts.append(jnp.zeros((4, LANES), jnp.float32))
        rows = jnp.concatenate(parts, axis=0)
        crow[e + 1] = rows
        start = pl.multiple_of(ess_start + e * LANES, LANES)
        cols[pl.ds(start, LANES), :] = jnp.transpose(rows)
        return carry

    loop(n_wide // slots, ess_rows, 0)

    if kicks == n_wide:
        shared = bodies
    else:
        shared = ess_start
        kicked = []
        for t in every:

            def one_block(k, acc):
                listed = star_leaf[t * leaves // tiles, k]
                start = bodies + listed * stars
                return loop(
                    stars // ROWS, lambda g, part: on_bodies(start + g * ROWS, (t,), part), acc
                )

            kicked.append(lax.fori_loop(0, kicks, one_block, (total[t],))[0])
        total = tuple(kicked)
    total = loop(
        (ess_start + n_wide * GROUPS - shared) // ROWS,
        lambda g, acc: on_bodies(shared + g * ROWS, every, acc),
        total,
        BODY_UNROLL,
    )
    for t in every:
        for c in range(3):
            piece = jnp.sum(total[t][c], axis=0, keepdims=True)
            spot = (slice(c, c + 1), slice(t * LANES, (t + 1) * LANES))
            out[spot] = gal_vel[spot] + time_step * piece

    rest = states.at[pl.ds(0, n_narrow - 1)]
    pltpu.make_async_copy(rest, rest, pass_recv_sem).wait()

    def passed_rows(i, carry):
        n = lax.rem(narrow + 1 + i // halves, n_narrow)
        star_rows(n, lax.rem(i, halves))
        return carry

    loop((n_narrow - 1) * halves, passed_rows, 0, 12)
    pairs = n_narrow * halves

    pieces = []
    for t in range(0, stars, ROWS):
        mine = targets[t : t + ROWS, :]
        place = [column(mine, c) for c in range(3)]
        speed = [column(mine, 4 + c) for c in range(3)]

        def hermite(i, acc):
            rows = [spread(srow[i, c : c + 1, :]) for c in range(7)]
            dx, dy, dz = (rows[c] - place[c] for c in range(3))
            ux, uy, uz = (rows[4 + c] - speed[c] for c in range(3))
            inverse = lax.rsqrt(dx * dx + dy * dy + dz * dz + soften_sq)
            square = inverse * inverse
            weight = rows[3] * inverse * square
            approach = 3.0 * (dx * ux + dy * uy + dz * uz) * square
            return (
                acc[0] + dx * weight,
                acc[1] + dy * weight,
                acc[2] + dz * weight,
                acc[3] + (ux - dx * approach) * weight,
                acc[4] + (uy - dy * approach) * weight,
                acc[5] + (uz - dz * approach) * weight,
            )

        acc = loop(pairs, hermite, (zero,) * 6, STAR_UNROLL)

        def cell_pull(i, part):
            rows = [spread(crow[i, c : c + 1, :]) for c in range(4)]
            return pull(rows[:3], rows[3], place, part)

        acc = loop(n_wide // slots + 1, cell_pull, acc[:3]) + acc[3:]
        piece = jnp.zeros((ROWS, LANES), jnp.float32)
        for c in range(6):
            piece = jnp.where(lane8 == c, jnp.sum(acc[c], axis=1, keepdims=True), piece)
        pieces.append(piece)
    result = jnp.transpose(jnp.concatenate(pieces, axis=0))
    new_acc, new_jerk = result[0:3], result[3:6]
    vel_new = (
        svel + time_step * 0.5 * (sacc + new_acc) + step_sq / 12.0 * (sjerk - new_jerk)
    )
    vel_at = bodies + LANES
    out[:, vel_at : vel_at + stars] = vel_new
    out[:, bodies : bodies + stars] = (
        spos + time_step * 0.5 * (svel + vel_new) + step_sq / 12.0 * (sacc - new_acc)
    )

    pltpu.make_async_copy(some, some, send_sem).wait()
    pltpu.make_async_copy(few, few, cell_send_sem).wait()
    pltpu.make_async_copy(rest, rest, pass_send_sem).wait()


def unpack(packed, gal_out, pos_out, vel_out):
    bodies, stars = gal_out.shape[1], pos_out.shape[1]
    gal_out[...] = packed[:, 0:bodies]
    pos_out[...] = packed[:, bodies : bodies + stars]
    vel_out[...] = packed[:, bodies + LANES : bodies + LANES + stars]


def body(
    n_wide,
    n_narrow,
    star_pos,
    star_vel,
    star_mass,
    star_acc,
    star_jerk,
    gal_pos,
    gal_vel,
    gal_mass,
    group_of,
    let_send,
    star_leaf,
):
    n_dev = n_wide * n_narrow
    stars, bodies = star_pos.shape[1], gal_pos.shape[1]
    vmem = pl.BlockSpec(memory_space=pltpu.VMEM)
    f32 = jnp.float32
    i32 = jnp.int32
    hbm = pl.BlockSpec(memory_space=pltpu.HBM)
    packed = pl.pallas_call(
        functools.partial(kernel, n_wide, n_narrow),
        out_shape=jax.ShapeDtypeStruct((3, bodies + 2 * LANES), f32),
        in_specs=[hbm] * 11,
        out_specs=vmem,
        scratch_shapes=[
            pltpu.VMEM((3, stars), f32),
            pltpu.VMEM((3, stars), f32),
            pltpu.VMEM((1, stars), f32),
            pltpu.VMEM((3, stars), f32),
            pltpu.VMEM((3, stars), f32),
            pltpu.VMEM((3, bodies), f32),
            pltpu.VMEM((3, bodies), f32),
            pltpu.VMEM((1, bodies), f32),
            pltpu.VMEM((1, bodies), i32),
            pltpu.VMEM((1, n_wide), i32),
            pltpu.SMEM(star_leaf.shape, i32),
            pltpu.SemaphoreType.DMA((11,)),
            pltpu.VMEM((n_narrow, n_wide, 4, LANES), f32),
            pltpu.VMEM((n_wide, 1, LANES), f32),
            pltpu.VMEM((n_wide, 1, LANES), f32),
            pltpu.VMEM((bodies + n_wide * (stars + GROUPS), ROWS), f32),
            pltpu.VMEM((n_dev // 2, ROWS, LANES), f32),
            pltpu.VMEM((n_wide * GROUPS // LANES + 1, ROWS, LANES), f32),
            pltpu.SemaphoreType.DMA,
            pltpu.SemaphoreType.DMA,
            pltpu.SemaphoreType.DMA,
            pltpu.SemaphoreType.DMA,
            pltpu.SemaphoreType.DMA,
            pltpu.SemaphoreType.DMA,
        ],
        compiler_params=pltpu.CompilerParams(
            collective_id=0, has_side_effects=True, vmem_limit_bytes=24 << 20
        ),
    )(
        *(
            pltpu.with_memory_space_constraint(array, pltpu.HBM)
            for array in (
                star_pos,
                star_vel,
                star_mass.reshape(1, stars),
                star_acc,
                star_jerk,
                gal_pos,
                gal_vel,
                gal_mass.reshape(1, bodies),
                group_of.reshape(1, bodies),
                let_send.reshape(1, n_wide),
                star_leaf,
            )
        )
    )
    return pl.pallas_call(
        unpack,
        out_shape=(
            jax.ShapeDtypeStruct(gal_vel.shape, f32),
            jax.ShapeDtypeStruct(star_pos.shape, f32),
            jax.ShapeDtypeStruct(star_vel.shape, f32),
        ),
        in_specs=[vmem],
        out_specs=(vmem,) * 3,
        compiler_params=pltpu.CompilerParams(vmem_limit_bytes=1 << 20),
    )(packed)


def solution(mesh):
    both = ("wide", "narrow")
    columns, flat = P(None, both), P(both)
    return jax.shard_map(
        functools.partial(body, mesh.shape["wide"], mesh.shape["narrow"]),
        mesh=mesh,
        in_specs=(
            columns,
            columns,
            flat,
            columns,
            columns,
            columns,
            columns,
            flat,
            flat,
            P(both, None, None),
            P(both, None),
        ),
        out_specs=(columns, columns, columns),
        check_vma=False,
    )
```

profile of v0, /device:TPU:0, one launch (start us, length us, event | category | flops | bytes accessed | tf_op | source)
XLA Modules:
  0.0 13.6 jit_solution(9504778887181297206)
XLA Ops:
  0.6 12.4 %shard_map.130.packed = f32[3,768]{1,0:T(4,128)S(1)} custom-call(f32[3,64]{1,0:T(4,128)} %star_pos_hbm.1, f32[3,64]{1,0:T(4,128)} %star_vel_hbm.1, f32[1,64]{1,0:T(1,128)} %bitcast.6, f32[3,64]{1,0:T(4,128)} %star_acc_hbm.1, f32[3,64]{1,0:T(4,128)} %star_jerk_hbm.1, f32[3,512]{1,0:T(4,128)} %gal_pos_hbm.1, f32[3,512]{1,0:T(4,128)} %gal_vel_hbm.1, ...), custom_call_target="tpu_custom_call" | custom-call | tf_op jit(solution)/shard_map/pallas_call | solution.py:416
  13.0 0.6 %shard_map.131 = (f32[3,512]{1,0:T(4,128)}, f32[3,64]{1,0:T(4,128)}, f32[3,64]{1,0:T(4,128)}) custom-call(f32[3,768]{1,0:T(4,128)S(1)} %shard_map.130.packed), custom_call_target="tpu_custom_call" | custom-call | tf_op jit(solution)/shard_map/pallas_call | solution.py:468
where the time goes:
time: 13.8 us; the launch traced here: 13.6 us
  Pallas kernels  13 us (94%)
  between operations  0.64 us (5%)
    pallas_call x1, Pallas kernels, body(): pl.pallas_call(functools.partial(kernel, n_wide, n_narrow), out_shape=jax...  12.4 us
    pallas_call x1, Pallas kernels, body(): pl.pallas_call(unpack, out_shape=(jax.ShapeDtypeStruct(gal_vel.shape, f32...  0.61 us

commit v1 on v0

--- a/solution.py
+++ b/solution.py
@@ -10,8 +10,7 @@
 GROUPS = 32
 LANES = 128
 ROWS = 8
-BODY_UNROLL = 32
-STAR_UNROLL = 16
+BODY_UNROLL = 16
 MESH = pl.DeviceIdType.MESH
 
 time_step = 0.25
@@ -70,13 +69,16 @@
     cell_in,
     cols,
     srow,
-    crow,
+    aims,
+    body_sum,
+    star_sum,
     send_sem,
-    recv_sem,
+    near_sem,
     cell_send_sem,
     cell_recv_sem,
     pass_send_sem,
     pass_recv_sem,
+    enter_sem,
 ):
     wide, narrow = lax.axis_index("wide"), lax.axis_index("narrow")
     stars = star_pos.shape[1]
@@ -84,6 +86,10 @@
     leaves, kicks = star_leaf.shape
     slots = LANES // GROUPS
     step_sq = time_step * time_step
+    tiles = bodies // LANES
+    every = tuple(range(tiles))
+    star_at = bodies
+    cell_at = bodies + n_wide * stars
 
     fetches = [
         pltpu.make_async_copy(source, target, in_sem.at[i])
@@ -103,28 +109,28 @@
             )
         )
     ]
-    barrier = pltpu.get_barrier_semaphore()
-
-    def greet(w, n):
-        pl.semaphore_signal(barrier, inc=1, device_id=(w, n), device_id_type=MESH)
-
-    beside = [narrow] + [lax.rem(narrow + m, n_narrow) for m in range(1, n_narrow)]
-
-    def each_wide(first, step):
-        lax.fori_loop(first, n_wide, step, 0, unroll=n_wide <= 16)
-
-    def greet_peers(j, carry):
-        w = lax.rem(wide + j, n_wide)
-        for n in beside:
-            greet(w, n)
-        return carry
-
-    each_wide(1, greet_peers)
-    for n in beside[1:]:
-        greet(wide, n)
-
     for fetch in fetches:
         fetch.start()
+
+    barrier = pltpu.get_barrier_semaphore()
+    others = [lax.rem(narrow + m, n_narrow) for m in range(1, n_narrow)]
+
+    def run(first, last, step):
+        def body(i, carry):
+            step(i)
+            return carry
+
+        lax.fori_loop(first, last, body, 0)
+
+    def signal(sem, w, n):
+        pl.semaphore_signal(sem, inc=1, device_id=(w, n), device_id_type=MESH)
+
+    def signal_group(sem, w):
+        for n in range(n_narrow):
+            signal(sem, w, n)
+
+    run(narrow + 1, n_narrow, lambda n: signal(barrier, wide, n))
+    run(wide + 1, n_wide, lambda w: signal_group(barrier, w))
 
     lane = lax.broadcasted_iota(jnp.int32, (1, LANES), 1)
     lane4 = lax.broadcasted_iota(jnp.int32, (4, LANES), 1)
@@ -132,7 +138,7 @@
     row8 = lax.broadcasted_iota(jnp.int32, (ROWS, LANES), 0)
     left = lane4 < stars
 
-    for fetch in fetches:
+    for fetch in fetches[:5]:
         fetch.wait()
 
     spos, svel = star_pos[...], star_vel[...]
@@ -146,10 +152,48 @@
     block = jnp.concatenate([pos4, vel4], axis=1)
     block = jnp.where(lax.rem(wide, 2) == 0, block, pltpu.roll(block, stars, 1))
     states[narrow, wide] = block
-    both = jnp.concatenate([pos4, vel4], axis=0)
-    targets = jnp.transpose(
-        jnp.concatenate([both, jnp.zeros((ROWS, LANES - stars), jnp.float32)], axis=1)
-    )
+
+    smaller = wide * n_narrow + narrow
+
+    @pl.when(smaller > 0)
+    def _():
+        pl.semaphore_wait(barrier, smaller)
+
+    def send_state(w, n, sends, recvs):
+        pltpu.make_async_remote_copy(
+            src_ref=states.at[narrow, wide],
+            dst_ref=states.at[narrow, wide],
+            send_sem=sends,
+            recv_sem=recvs.at[wide],
+            device_id=(w, n),
+            device_id_type=MESH,
+        ).start()
+
+    def send_group(w):
+        send_state(w, narrow, send_sem, near_sem)
+        for n in others:
+            send_state(w, n, pass_send_sem, pass_recv_sem)
+
+    def send_beside(n):
+        send_state(wide, n, pass_send_sem, pass_recv_sem)
+
+    def send_cells(w):
+        pltpu.make_async_remote_copy(
+            src_ref=cell_out.at[w],
+            dst_ref=cell_in.at[wide],
+            send_sem=cell_send_sem,
+            recv_sem=cell_recv_sem.at[wide],
+            device_id=(w, narrow),
+            device_id_type=MESH,
+        ).start()
+
+    run(0, wide, send_group)
+    run(0, narrow, send_beside)
+    run(0, wide, lambda w: signal_group(enter_sem.at[wide], w))
+    run(0, narrow, lambda n: signal(enter_sem.at[wide], wide, n))
+
+    for fetch in fetches[5:]:
+        fetch.wait()
 
     gpos, gmass = gal_pos[...], gal_mass[...]
     body_lane = lax.broadcasted_iota(jnp.int32, (1, bodies), 1)
@@ -169,7 +213,6 @@
         preferred_element_type=jnp.float32,
     )
     cells = jnp.where(row8 < 3, sums / spread(sums[3:4]), sums)
-    crow[0] = cells
 
     group = lane // GROUPS
     part = jnp.bitwise_and(group - lax.rem(wide, slots), slots - 1)
@@ -194,55 +237,24 @@
         )
     cell_out[:, 0, :] = outgoing
     cell_in[wide] = jnp.zeros((1, LANES), jnp.float32)
-
-    pl.semaphore_wait(barrier, n_wide * n_narrow - 1)
-
-    def send_state(w, n, sends, recvs):
-        pltpu.make_async_remote_copy(
-            src_ref=states.at[narrow, wide],
-            dst_ref=states.at[narrow, wide],
-            send_sem=sends,
-            recv_sem=recvs,
-            device_id=(w, n),
-            device_id_type=MESH,
-        ).start()
-
-    def send_wide(j, carry):
-        w = lax.rem(wide + j, n_wide)
-        pltpu.make_async_remote_copy(
-            src_ref=cell_out.at[w],
-            dst_ref=cell_in.at[wide],
-            send_sem=cell_send_sem,
-            recv_sem=cell_recv_sem,
-            device_id=(w, narrow),
-            device_id_type=MESH,
-        ).start()
-        send_state(w, narrow, send_sem, recv_sem)
-        return carry
-
-    def send_others(j, carry):
-        w = lax.rem(wide + j, n_wide)
-        for n in beside[1:]:
-            send_state(w, n, pass_send_sem, pass_recv_sem)
-        return carry
-
-    each_wide(1, send_wide)
-    each_wide(1, send_others)
-    for n in beside[1:]:
-        send_state(wide, n, pass_send_sem, pass_recv_sem)
-
-    tiles = bodies // LANES
+    run(0, wide, send_cells)
+
+    both = jnp.concatenate([pos4, vel4], axis=0)
+    targets = jnp.transpose(
+        jnp.concatenate([both, jnp.zeros((ROWS, LANES - stars), jnp.float32)], axis=1)
+    )
     body_rows = jnp.concatenate(
         [gpos, gmass, jnp.zeros((4, bodies), jnp.float32)], axis=0
     )
-    for t in range(tiles):
+    for t in every:
         cols[t * LANES : (t + 1) * LANES, :] = jnp.transpose(
             body_rows[:, t * LANES : (t + 1) * LANES]
         )
     here = [
         [spread(gpos[c : c + 1, t * LANES : (t + 1) * LANES]) for c in range(3)]
-        for t in range(tiles)
+        for t in every
     ]
+    zero = jnp.zeros((ROWS, LANES), jnp.float32)
 
     def on_bodies(start, which, total):
         source = cols[pl.ds(pl.multiple_of(start, ROWS), ROWS), :]
@@ -250,124 +262,173 @@
         mass = column(source, 3)
         return tuple(pull(place, mass, here[t], total[i]) for i, t in enumerate(which))
 
-    every = tuple(range(tiles))
-    zero = jnp.zeros((ROWS, LANES), jnp.float32)
-    total = tuple((zero, zero, zero) for _ in every)
-    total = loop(bodies // ROWS, lambda g, acc: on_bodies(g * ROWS, every, acc), total, BODY_UNROLL)
-
-    some = states.at[0, pl.ds(0, n_wide - 1)]
-    pltpu.make_async_copy(some, some, recv_sem).wait()
-    few = cell_in.at[pl.ds(0, n_wide - 1)]
-    pltpu.make_async_copy(few, few, cell_recv_sem).wait()
+    def keep(total):
+        for t in every:
+            for c in range(3):
+                body_sum[3 * t + c] = total[t][c]
+
+    def kept():
+        return tuple(tuple(body_sum[3 * t + c] for c in range(3)) for t in every)
+
+    def sweep(start, count, total):
+        return loop(
+            count // ROWS,
+            lambda g, acc: on_bodies(start + g * ROWS, every, acc),
+            total,
+            BODY_UNROLL,
+        )
+
+    def cells_on_stars(rows, t):
+        place = [aims[t, c] for c in range(3)]
+        return pull(rows[:3], rows[3], place, [star_sum[t, c] for c in range(3)])
+
+    own = [spread(cells[c : c + 1, :]) for c in range(4)]
+    star_groups = stars // ROWS
+    for t in range(star_groups):
+        mine = targets[t * ROWS : (t + 1) * ROWS, :]
+        place = [column(mine, c) for c in range(3)]
+        for c in range(3):
+            aims[t, c] = place[c]
+            aims[t, 3 + c] = column(mine, 4 + c)
+            star_sum[t, 3 + c] = zero
+        for c, value in enumerate(pull(own[:3], own[3], place, (zero,) * 3)):
+            star_sum[t, c] = value
+
+    keep(sweep(0, bodies, ((zero,) * 3,) * tiles))
+
+    def answer(w):
+        @pl.when(w == wide)
+        def _():
+            @pl.when(narrow < n_narrow - 1)
+            def _():
+                pl.semaphore_wait(enter_sem.at[wide], n_narrow - 1 - narrow)
+
+            run(narrow + 1, n_narrow, send_beside)
+
+        @pl.when(w > wide)
+        def _():
+            pl.semaphore_wait(enter_sem.at[w], n_narrow)
+            send_group(w)
+            send_cells(w)
+
     halves = n_wide // 2
-
-    def star_rows(n, i):
-        even_block, odd_block = states[n, 2 * i], states[n, 2 * i + 1]
+    lower = wide < halves
+
+    run(wide, n_wide, answer)
+
+    def gather(n, even):
+        even_block, odd_block = states[n, even], states[n, even + 1]
         rows = jnp.where(left, even_block, odd_block)
-        spot = n * halves + i
-        srow[spot, 0:4, :] = rows
-        srow[spot, 4:8, :] = pltpu.roll(jnp.where(left, odd_block, even_block), stars, 1)
-        return rows
-
-    def star_cols(i, carry):
-        rows = jnp.concatenate(
-            [star_rows(narrow, i), jnp.zeros((4, LANES), jnp.float32)], axis=0
-        )
-        start = pl.multiple_of(bodies + i * LANES, LANES)
+        speeds = pltpu.roll(jnp.where(left, odd_block, even_block), stars, 1)
+        return rows, speeds
+
+    def arrived(ref, sem, w):
+        @pl.when(w != wide)
+        def _():
+            pltpu.make_async_copy(ref, ref, sem.at[w]).wait()
+
+    def near_stars(even):
+        for w in (even, even + 1):
+            arrived(states.at[0, 0], near_sem, w)
+        rows, _ = gather(narrow, even)
+        rows = jnp.concatenate([rows, jnp.zeros((4, LANES), jnp.float32)], axis=0)
+        start = pl.multiple_of(star_at + even * stars, LANES)
         cols[pl.ds(start, LANES), :] = jnp.transpose(rows)
-        return carry
-
-    loop(halves, star_cols, 0)
-    ess_start = bodies + n_wide * stars
-
-    def ess_rows(e, carry):
+        if kicks == n_wide:
+            keep(sweep(start, LANES, kept()))
+
+    def near_cells(e):
+        for k in range(slots):
+            arrived(cell_in.at[0], cell_recv_sem, e * slots + k)
         parts = []
         for c in range(4):
             row = jnp.zeros((1, LANES), jnp.float32)
             for k in range(slots):
                 row = jnp.where(group == (c + k) % slots, cell_in[e * slots + k], row)
             parts.append(row if c == 0 else pltpu.roll(row, LANES - c * GROUPS, 1))
+        rows = [spread(part) for part in parts]
+        for t in range(star_groups):
+            for c, value in enumerate(cells_on_stars(rows, t)):
+                star_sum[t, c] = value
         parts.append(jnp.zeros((4, LANES), jnp.float32))
-        rows = jnp.concatenate(parts, axis=0)
-        crow[e + 1] = rows
-        start = pl.multiple_of(ess_start + e * LANES, LANES)
-        cols[pl.ds(start, LANES), :] = jnp.transpose(rows)
-        return carry
-
-    loop(n_wide // slots, ess_rows, 0)
-
-    if kicks == n_wide:
-        shared = bodies
-    else:
-        shared = ess_start
+        start = pl.multiple_of(cell_at + e * LANES, LANES)
+        cols[pl.ds(start, LANES), :] = jnp.transpose(jnp.concatenate(parts, axis=0))
+        keep(sweep(start, LANES, kept()))
+
+    def all_stars(even):
+        for w in (even, even + 1):
+            few = states.at[pl.ds(0, n_narrow - 1), 0]
+            pltpu.make_async_copy(few, few, pass_recv_sem.at[w]).wait()
+        for n in range(n_narrow):
+            rows, speeds = gather(n, even)
+            srow[n, 0:4, :] = rows
+            srow[n, 4:8, :] = speeds
+        sources = [
+            [spread(srow[n, c : c + 1, :]) for c in range(7)] for n in range(n_narrow)
+        ]
+        for t in range(star_groups):
+            place = [aims[t, c] for c in range(3)]
+            speed = [aims[t, 3 + c] for c in range(3)]
+            acc = [star_sum[t, c] for c in range(6)]
+            for rows in sources:
+                dx, dy, dz = (rows[c] - place[c] for c in range(3))
+                ux, uy, uz = (rows[4 + c] - speed[c] for c in range(3))
+                inverse = lax.rsqrt(dx * dx + dy * dy + dz * dz + soften_sq)
+                square = inverse * inverse
+                weight = rows[3] * inverse * square
+                approach = 3.0 * (dx * ux + dy * uy + dz * uz) * square
+                acc = [
+                    acc[0] + dx * weight,
+                    acc[1] + dy * weight,
+                    acc[2] + dz * weight,
+                    acc[3] + (ux - dx * approach) * weight,
+                    acc[4] + (uy - dy * approach) * weight,
+                    acc[5] + (uz - dz * approach) * weight,
+                ]
+            for c in range(6):
+                star_sum[t, c] = acc[c]
+
+    pairs_per_row = slots // 2
+
+    def turn(p):
+        q = jnp.where(lower, p, halves - 1 - p)
+        near_stars(2 * q)
+
+        @pl.when(lax.rem(p, pairs_per_row) == pairs_per_row - 1)
+        def _():
+            near_cells(q // pairs_per_row)
+
+        all_stars(2 * q)
+
+    run(0, halves, turn)
+
+    total = kept()
+    if kicks != n_wide:
         kicked = []
         for t in every:
 
             def one_block(k, acc):
                 listed = star_leaf[t * leaves // tiles, k]
-                start = bodies + listed * stars
+                start = star_at + listed * stars
                 return loop(
                     stars // ROWS, lambda g, part: on_bodies(start + g * ROWS, (t,), part), acc
                 )
 
             kicked.append(lax.fori_loop(0, kicks, one_block, (total[t],))[0])
         total = tuple(kicked)
-    total = loop(
-        (ess_start + n_wide * GROUPS - shared) // ROWS,
-        lambda g, acc: on_bodies(shared + g * ROWS, every, acc),
-        total,
-        BODY_UNROLL,
-    )
     for t in every:
         for c in range(3):
             piece = jnp.sum(total[t][c], axis=0, keepdims=True)
             spot = (slice(c, c + 1), slice(t * LANES, (t + 1) * LANES))
             out[spot] = gal_vel[spot] + time_step * piece
 
-    rest = states.at[pl.ds(0, n_narrow - 1)]
-    pltpu.make_async_copy(rest, rest, pass_recv_sem).wait()
-
-    def passed_rows(i, carry):
-        n = lax.rem(narrow + 1 + i // halves, n_narrow)
-        star_rows(n, lax.rem(i, halves))
-        return carry
-
-    loop((n_narrow - 1) * halves, passed_rows, 0, 12)
-    pairs = n_narrow * halves
-
     pieces = []
-    for t in range(0, stars, ROWS):
-        mine = targets[t : t + ROWS, :]
-        place = [column(mine, c) for c in range(3)]
-        speed = [column(mine, 4 + c) for c in range(3)]
-
-        def hermite(i, acc):
-            rows = [spread(srow[i, c : c + 1, :]) for c in range(7)]
-            dx, dy, dz = (rows[c] - place[c] for c in range(3))
-            ux, uy, uz = (rows[4 + c] - speed[c] for c in range(3))
-            inverse = lax.rsqrt(dx * dx + dy * dy + dz * dz + soften_sq)
-            square = inverse * inverse
-            weight = rows[3] * inverse * square
-            approach = 3.0 * (dx * ux + dy * uy + dz * uz) * square
-            return (
-                acc[0] + dx * weight,
-                acc[1] + dy * weight,
-                acc[2] + dz * weight,
-                acc[3] + (ux - dx * approach) * weight,
-                acc[4] + (uy - dy * approach) * weight,
-                acc[5] + (uz - dz * approach) * weight,
-            )
-
-        acc = loop(pairs, hermite, (zero,) * 6, STAR_UNROLL)
-
-        def cell_pull(i, part):
-            rows = [spread(crow[i, c : c + 1, :]) for c in range(4)]
-            return pull(rows[:3], rows[3], place, part)
-
-        acc = loop(n_wide // slots + 1, cell_pull, acc[:3]) + acc[3:]
+    for t in range(star_groups):
         piece = jnp.zeros((ROWS, LANES), jnp.float32)
         for c in range(6):
-            piece = jnp.where(lane8 == c, jnp.sum(acc[c], axis=1, keepdims=True), piece)
+            piece = jnp.where(
+                lane8 == c, jnp.sum(star_sum[t, c], axis=1, keepdims=True), piece
+            )
         pieces.append(piece)
     result = jnp.transpose(jnp.concatenate(pieces, axis=0))
     new_acc, new_jerk = result[0:3], result[3:6]
@@ -380,6 +441,9 @@
         spos + time_step * 0.5 * (svel + vel_new) + step_sq / 12.0 * (sacc - new_acc)
     )
 
+    some = states.at[0, pl.ds(0, n_wide - 1)]
+    few = cell_in.at[pl.ds(0, n_wide - 1)]
+    rest = states.at[pl.ds(0, n_narrow - 1)]
     pltpu.make_async_copy(some, some, send_sem).wait()
     pltpu.make_async_copy(few, few, cell_send_sem).wait()
     pltpu.make_async_copy(rest, rest, pass_send_sem).wait()
@@ -407,7 +471,6 @@
     let_send,
     star_leaf,
 ):
-    n_dev = n_wide * n_narrow
     stars, bodies = star_pos.shape[1], gal_pos.shape[1]
     vmem = pl.BlockSpec(memory_space=pltpu.VMEM)
     f32 = jnp.float32
@@ -435,14 +498,17 @@
             pltpu.VMEM((n_wide, 1, LANES), f32),
             pltpu.VMEM((n_wide, 1, LANES), f32),
             pltpu.VMEM((bodies + n_wide * (stars + GROUPS), ROWS), f32),
-            pltpu.VMEM((n_dev // 2, ROWS, LANES), f32),
-            pltpu.VMEM((n_wide * GROUPS // LANES + 1, ROWS, LANES), f32),
+            pltpu.VMEM((n_narrow, ROWS, LANES), f32),
+            pltpu.VMEM((stars // ROWS, 6, ROWS, LANES), f32),
+            pltpu.VMEM((3 * bodies // LANES, ROWS, LANES), f32),
+            pltpu.VMEM((stars // ROWS, 6, ROWS, LANES), f32),
             pltpu.SemaphoreType.DMA,
+            pltpu.SemaphoreType.DMA((n_wide,)),
             pltpu.SemaphoreType.DMA,
+            pltpu.SemaphoreType.DMA((n_wide,)),
             pltpu.SemaphoreType.DMA,
-            pltpu.SemaphoreType.DMA,
-            pltpu.SemaphoreType.DMA,
-            pltpu.SemaphoreType.DMA,
+            pltpu.SemaphoreType.DMA((n_wide,)),
+            pltpu.SemaphoreType.REGULAR((n_wide,)),
         ],
         compiler_params=pltpu.CompilerParams(
             collective_id=0, has_side_effects=True, vmem_limit_bytes=24 << 20

time: 13.8 us -> 12.9 us (0.935)
  Pallas kernels: 13 us -> 12.1 us
    pallas_call x1, Pallas kernels: 12.4 us -> 11.5 us  [body(): pl.pallas_call(functools.partial(kernel, n_wide, n_narrow), out_shape=jax...]
where the time goes in v1:
time: 12.9 us; the launch traced here: 12.8 us
  Pallas kernels  12.1 us (94%)
  between operations  0.64 us (5%)
    pallas_call x1, Pallas kernels, body(): pl.pallas_call(functools.partial(kernel, n_wide, n_narrow), out_shape=jax...  11.5 us
    pallas_call x1, Pallas kernels, body(): pl.pallas_call(unpack, out_shape=(jax.ShapeDtypeStruct(gal_vel.shape, f32...  0.61 us

profile of v1, /device:TPU:0, one launch (start us, length us, event | category | flops | bytes accessed | tf_op | source)
XLA Modules:
  0.0 12.8 jit_solution(15052135463125538574)
XLA Ops:
  0.6 11.5 %shard_map.130.packed = f32[3,768]{1,0:T(4,128)S(1)} custom-call(f32[3,64]{1,0:T(4,128)} %star_pos_hbm.1, f32[3,64]{1,0:T(4,128)} %star_vel_hbm.1, f32[1,64]{1,0:T(1,128)} %bitcast.6, f32[3,64]{1,0:T(4,128)} %star_acc_hbm.1, f32[3,64]{1,0:T(4,128)} %star_jerk_hbm.1, f32[3,512]{1,0:T(4,128)} %gal_pos_hbm.1, f32[3,512]{1,0:T(4,128)} %gal_vel_hbm.1, ...), custom_call_target="tpu_custom_call" | custom-call | tf_op jit(solution)/shard_map/pallas_call | solution.py:479
  12.2 0.6 %shard_map.131 = (f32[3,512]{1,0:T(4,128)}, f32[3,64]{1,0:T(4,128)}, f32[3,64]{1,0:T(4,128)}) custom-call(f32[3,768]{1,0:T(4,128)S(1)} %shard_map.130.packed), custom_call_target="tpu_custom_call" | custom-call | tf_op jit(solution)/shard_map/pallas_call | solution.py:534

commit v2 on v1

--- a/solution.py
+++ b/solution.py
@@ -187,10 +187,12 @@
             device_id_type=MESH,
         ).start()
 
-    run(0, wide, send_group)
-    run(0, narrow, send_beside)
+    first = jnp.minimum(wide, 1)
+    run(0, first, send_group)
     run(0, wide, lambda w: signal_group(enter_sem.at[wide], w))
     run(0, narrow, lambda n: signal(enter_sem.at[wide], wide, n))
+    run(first, wide, send_group)
+    run(0, narrow, send_beside)
 
     for fetch in fetches[5:]:
         fetch.wait()
@@ -312,9 +314,8 @@
             send_cells(w)
 
     halves = n_wide // 2
-    lower = wide < halves
-
-    run(wide, n_wide, answer)
+    lower = wide < n_wide // 4
+
 
     def gather(n, even):
         even_block, odd_block = states[n, even], states[n, even + 1]
@@ -390,7 +391,14 @@
 
     pairs_per_row = slots // 2
 
+    early = jnp.where(lower, halves, n_wide)
+
     def turn(p):
+        run(
+            jnp.where(p == 0, wide, early),
+            jnp.where(p == 0, early, jnp.where(p == 1, n_wide, 0)),
+            answer,
+        )
         q = jnp.where(lower, p, halves - 1 - p)
         near_stars(2 * q)
 

time: 12.9 us -> 12.5 us (0.969)
  Pallas kernels: 12.1 us -> 11.7 us
    pallas_call x1, Pallas kernels: 11.5 us -> 11.1 us  [body(): pl.pallas_call(functools.partial(kernel, n_wide, n_narrow), out_shape=jax...]
where the time goes in v2:
time: 12.5 us; the launch traced here: 12.3 us
  Pallas kernels  11.7 us (94%)
  between operations  0.64 us (5%)
    pallas_call x1, Pallas kernels, body(): pl.pallas_call(functools.partial(kernel, n_wide, n_narrow), out_shape=jax...  11.1 us
    pallas_call x1, Pallas kernels, body(): pl.pallas_call(unpack, out_shape=(jax.ShapeDtypeStruct(gal_vel.shape, f32...  0.61 us

profile of v2, /device:TPU:0, one launch (start us, length us, event | category | flops | bytes accessed | tf_op | source)
XLA Modules:
  0.0 12.3 jit_solution(8388947604868142235)
XLA Ops:
  0.6 11.1 %shard_map.130.packed = f32[3,768]{1,0:T(4,128)S(1)} custom-call(f32[3,64]{1,0:T(4,128)} %star_pos_hbm.1, f32[3,64]{1,0:T(4,128)} %star_vel_hbm.1, f32[1,64]{1,0:T(1,128)} %bitcast.6, f32[3,64]{1,0:T(4,128)} %star_acc_hbm.1, f32[3,64]{1,0:T(4,128)} %star_jerk_hbm.1, f32[3,512]{1,0:T(4,128)} %gal_pos_hbm.1, f32[3,512]{1,0:T(4,128)} %gal_vel_hbm.1, ...), custom_call_target="tpu_custom_call" | custom-call | tf_op jit(solution)/shard_map/pallas_call | solution.py:487
  11.7 0.6 %shard_map.131 = (f32[3,512]{1,0:T(4,128)}, f32[3,64]{1,0:T(4,128)}, f32[3,64]{1,0:T(4,128)}) custom-call(f32[3,768]{1,0:T(4,128)S(1)} %shard_map.130.packed), custom_call_target="tpu_custom_call" | custom-call | tf_op jit(solution)/shard_map/pallas_call | solution.py:542

commit v3 on v2

--- a/solution.py
+++ b/solution.py
@@ -10,7 +10,6 @@
 GROUPS = 32
 LANES = 128
 ROWS = 8
-BODY_UNROLL = 16
 MESH = pl.DeviceIdType.MESH
 
 time_step = 0.25
@@ -35,6 +34,18 @@
     inverse = lax.rsqrt(dx * dx + dy * dy + dz * dz + soften_sq)
     weight = mass * inverse * inverse * inverse
     return (total[0] + dx * weight, total[1] + dy * weight, total[2] + dz * weight)
+
+
+def norm(rows):
+    return rows[0:1] * rows[0:1] + rows[1:2] * rows[1:2] + rows[2:3] * rows[2:3]
+
+
+def split(value):
+    parts = []
+    for _ in range(3):
+        parts.append(value.astype(jnp.bfloat16).astype(jnp.float32))
+        value = value - parts[-1]
+    return parts
 
 
 def kernel(
@@ -65,8 +76,10 @@
     star_leaf,
     in_sem,
     states,
+    cell_own,
     cell_out,
     cell_in,
+    aimed,
     cols,
     srow,
     aims,
@@ -88,8 +101,6 @@
     step_sq = time_step * time_step
     tiles = bodies // LANES
     every = tuple(range(tiles))
-    star_at = bodies
-    cell_at = bodies + n_wide * stars
 
     fetches = [
         pltpu.make_async_copy(source, target, in_sem.at[i])
@@ -153,12 +164,6 @@
     block = jnp.where(lax.rem(wide, 2) == 0, block, pltpu.roll(block, stars, 1))
     states[narrow, wide] = block
 
-    smaller = wide * n_narrow + narrow
-
-    @pl.when(smaller > 0)
-    def _():
-        pl.semaphore_wait(barrier, smaller)
-
     def send_state(w, n, sends, recvs):
         pltpu.make_async_remote_copy(
             src_ref=states.at[narrow, wide],
@@ -187,104 +192,100 @@
             device_id_type=MESH,
         ).start()
 
-    first = jnp.minimum(wide, 1)
-    run(0, first, send_group)
-    run(0, wide, lambda w: signal_group(enter_sem.at[wide], w))
-    run(0, narrow, lambda n: signal(enter_sem.at[wide], wide, n))
-    run(first, wide, send_group)
-    run(0, narrow, send_beside)
-
-    for fetch in fetches[5:]:
-        fetch.wait()
+    group = lane // GROUPS
+
+    def meet():
+        smaller = wide * n_narrow + narrow
+
+        @pl.when(smaller > 0)
+        def _():
+            pl.semaphore_wait(barrier, smaller)
+
+        run(0, wide, lambda w: signal_group(enter_sem.at[wide], w))
+        run(0, narrow, lambda n: signal(enter_sem.at[wide], wide, n))
+
+        def send_down(w):
+            send_group(w)
+
+            @pl.when(cells_first)
+            def _():
+                send_cells(w)
+
+        run(0, wide, send_down)
+        run(0, narrow, send_beside)
+
+    def make_cells():
+        for fetch in fetches[5:]:
+            fetch.wait()
+        gpos, gmass = gal_pos[...], gal_mass[...]
+        body_lane = lax.broadcasted_iota(jnp.int32, (1, bodies), 1)
+        segment = group_of[...] + (body_lane // (bodies // leaves)) * GROUPS
+        onehot = (
+            lax.broadcasted_iota(jnp.int32, (LANES, bodies), 0)
+            == jnp.broadcast_to(segment, (LANES, bodies))
+        ).astype(jnp.bfloat16)
+        moments = jnp.concatenate(
+            [gpos * gmass, gmass, jnp.zeros((4, bodies), jnp.float32)], axis=0
+        )
+        sums = lax.dot_general(
+            jnp.concatenate(split(moments), axis=0).astype(jnp.bfloat16),
+            onehot,
+            (((1,), (1,)), ((), ())),
+            preferred_element_type=jnp.float32,
+        )
+        sums = sums[0:8] + sums[8:16] + sums[16:24]
+        cells = jnp.where(row8 < 3, sums / spread(sums[3:4]), sums)
+        cell_own[...] = cells
+
+        part = jnp.bitwise_and(group - lax.rem(wide, slots), slots - 1)
+        square = (n_wide, n_wide)
+        diagonal = lax.broadcasted_iota(jnp.int32, square, 0) == lax.broadcasted_iota(
+            jnp.int32, square, 1
+        )
+        listed = jnp.broadcast_to(let_send[...].astype(jnp.float32), square)
+        chosen = jnp.sum(jnp.where(diagonal, listed, 0.0), axis=1, keepdims=True)
+        chosen = jnp.broadcast_to(chosen, (n_wide, LANES)).astype(jnp.int32)
+        outgoing = jnp.zeros((n_wide, LANES), jnp.float32)
+        pick = jnp.bitwise_and(group - chosen, slots - 1)
+        for k in range(slots):
+            turned = cells if k == 0 else pltpu.roll(cells, k * GROUPS, 1)
+            base = jnp.zeros((1, LANES), jnp.float32)
+            for c in range(4):
+                base = jnp.where(part == c, turned[c : c + 1], base)
+            outgoing = jnp.where(
+                jnp.logical_and(pick == k, chosen >= 0),
+                jnp.broadcast_to(base, (n_wide, LANES)),
+                outgoing,
+            )
+        cell_out[:, 0, :] = outgoing
+        cell_in[wide] = jnp.zeros((1, LANES), jnp.float32)
+
+    cells_first = jnp.logical_or(lax.rem(wide, 2) == 0, narrow < n_narrow // 2)
+
+    def order(i):
+        @pl.when(jnp.equal(i == 0, cells_first))
+        def _():
+            make_cells()
+
+        @pl.when(jnp.not_equal(i == 0, cells_first))
+        def _():
+            meet()
+
+    run(0, 2, order)
+
+    @pl.when(jnp.logical_not(cells_first))
+    def _():
+        run(0, wide, send_cells)
 
     gpos, gmass = gal_pos[...], gal_mass[...]
-    body_lane = lax.broadcasted_iota(jnp.int32, (1, bodies), 1)
-    segment = group_of[...] + (body_lane // (bodies // leaves)) * GROUPS
-    onehot = (
-        lax.broadcasted_iota(jnp.int32, (LANES, bodies), 0)
-        == jnp.broadcast_to(segment, (LANES, bodies))
-    ).astype(jnp.float32)
-    moments = jnp.concatenate(
-        [gpos * gmass, gmass, jnp.zeros((4, bodies), jnp.float32)], axis=0
-    )
-    sums = lax.dot_general(
-        moments,
-        onehot,
-        (((1,), (1,)), ((), ())),
-        precision=lax.Precision.HIGHEST,
-        preferred_element_type=jnp.float32,
-    )
-    cells = jnp.where(row8 < 3, sums / spread(sums[3:4]), sums)
-
-    group = lane // GROUPS
-    part = jnp.bitwise_and(group - lax.rem(wide, slots), slots - 1)
-    square = (n_wide, n_wide)
-    diagonal = lax.broadcasted_iota(jnp.int32, square, 0) == lax.broadcasted_iota(
-        jnp.int32, square, 1
-    )
-    listed = jnp.broadcast_to(let_send[...].astype(jnp.float32), square)
-    chosen = jnp.sum(jnp.where(diagonal, listed, 0.0), axis=1, keepdims=True)
-    chosen = jnp.broadcast_to(chosen, (n_wide, LANES)).astype(jnp.int32)
-    outgoing = jnp.zeros((n_wide, LANES), jnp.float32)
-    pick = jnp.bitwise_and(group - chosen, slots - 1)
-    for k in range(slots):
-        turned = cells if k == 0 else pltpu.roll(cells, k * GROUPS, 1)
-        base = jnp.zeros((1, LANES), jnp.float32)
-        for c in range(4):
-            base = jnp.where(part == c, turned[c : c + 1], base)
-        outgoing = jnp.where(
-            jnp.logical_and(pick == k, chosen >= 0),
-            jnp.broadcast_to(base, (n_wide, LANES)),
-            outgoing,
-        )
-    cell_out[:, 0, :] = outgoing
-    cell_in[wide] = jnp.zeros((1, LANES), jnp.float32)
-    run(0, wide, send_cells)
 
     both = jnp.concatenate([pos4, vel4], axis=0)
     targets = jnp.transpose(
         jnp.concatenate([both, jnp.zeros((ROWS, LANES - stars), jnp.float32)], axis=1)
     )
-    body_rows = jnp.concatenate(
-        [gpos, gmass, jnp.zeros((4, bodies), jnp.float32)], axis=0
-    )
-    for t in every:
-        cols[t * LANES : (t + 1) * LANES, :] = jnp.transpose(
-            body_rows[:, t * LANES : (t + 1) * LANES]
-        )
-    here = [
-        [spread(gpos[c : c + 1, t * LANES : (t + 1) * LANES]) for c in range(3)]
-        for t in every
-    ]
     zero = jnp.zeros((ROWS, LANES), jnp.float32)
 
-    def on_bodies(start, which, total):
-        source = cols[pl.ds(pl.multiple_of(start, ROWS), ROWS), :]
-        place = [column(source, c) for c in range(3)]
-        mass = column(source, 3)
-        return tuple(pull(place, mass, here[t], total[i]) for i, t in enumerate(which))
-
-    def keep(total):
-        for t in every:
-            for c in range(3):
-                body_sum[3 * t + c] = total[t][c]
-
-    def kept():
-        return tuple(tuple(body_sum[3 * t + c] for c in range(3)) for t in every)
-
-    def sweep(start, count, total):
-        return loop(
-            count // ROWS,
-            lambda g, acc: on_bodies(start + g * ROWS, every, acc),
-            total,
-            BODY_UNROLL,
-        )
-
-    def cells_on_stars(rows, t):
-        place = [aims[t, c] for c in range(3)]
-        return pull(rows[:3], rows[3], place, [star_sum[t, c] for c in range(3)])
-
-    own = [spread(cells[c : c + 1, :]) for c in range(4)]
+    own = [spread(cell_own[c : c + 1, :]) for c in range(4)]
     star_groups = stars // ROWS
     for t in range(star_groups):
         mine = targets[t * ROWS : (t + 1) * ROWS, :]
@@ -296,7 +297,58 @@
         for c, value in enumerate(pull(own[:3], own[3], place, (zero,) * 3)):
             star_sum[t, c] = value
 
-    keep(sweep(0, bodies, ((zero,) * 3,) * tiles))
+    last4 = lax.broadcasted_iota(jnp.int32, (4, bodies), 0) == 3
+    high, mid, low = split(jnp.concatenate([-2.0 * gpos, jnp.zeros_like(gmass)], axis=0))
+    high = jnp.where(last4, 1.0, high)
+    reach = split(norm(gpos) + soften_sq)
+    blank = jnp.zeros_like(gmass)
+    aimed[...] = jnp.concatenate(
+        [high, mid, high, low, high, mid, *reach, blank, blank, blank, blank, blank],
+        axis=0,
+    ).astype(jnp.bfloat16)
+
+    def on_bodies(rows, total):
+        square = norm(rows[0:3])
+        high, mid, low = split(jnp.concatenate([rows[0:3], square], axis=0))
+        ones = jnp.ones((4, LANES), jnp.float32)
+        turned = jnp.transpose(
+            jnp.concatenate([high, high, mid, high, low, mid, ones, rows], axis=0)
+        )
+        reach = jnp.dot(
+            turned.astype(jnp.bfloat16), aimed[...], preferred_element_type=jnp.float32
+        )
+        total = [list(part) for part in total]
+        for g in range(LANES // ROWS):
+            mine = turned[g * ROWS : (g + 1) * ROWS, :]
+            place = [column(mine, 28 + c) for c in range(3)]
+            mass = column(mine, 31)
+            for t in every:
+                inverse = lax.rsqrt(
+                    reach[g * ROWS : (g + 1) * ROWS, t * LANES : (t + 1) * LANES]
+                )
+                weight = mass * inverse * (inverse * inverse)
+                for c in range(3):
+                    total[t][c] = total[t][c] + place[c] * weight
+                total[t][3] = total[t][3] + weight
+        return total
+
+    def keep(total):
+        for t in every:
+            for c in range(4):
+                body_sum[4 * t + c] = total[t][c]
+
+    def kept():
+        return [[body_sum[4 * t + c] for c in range(4)] for t in every]
+
+    def cells_on_stars(rows, t):
+        place = [aims[t, c] for c in range(3)]
+        return pull(rows[:3], rows[3], place, [star_sum[t, c] for c in range(3)])
+
+    total = [[zero] * 4 for _ in every]
+    for t in every:
+        tile = slice(t * LANES, (t + 1) * LANES)
+        total = on_bodies(jnp.concatenate([gpos[:, tile], gmass[:, tile]], axis=0), total)
+    keep(total)
 
     def answer(w):
         @pl.when(w == wide)
@@ -328,19 +380,15 @@
         def _():
             pltpu.make_async_copy(ref, ref, sem.at[w]).wait()
 
-    def near_stars(even):
-        for w in (even, even + 1):
-            arrived(states.at[0, 0], near_sem, w)
-        rows, _ = gather(narrow, even)
-        rows = jnp.concatenate([rows, jnp.zeros((4, LANES), jnp.float32)], axis=0)
-        start = pl.multiple_of(star_at + even * stars, LANES)
-        cols[pl.ds(start, LANES), :] = jnp.transpose(rows)
+    def near_stars(even, total):
+        near, _ = gather(narrow, even)
         if kicks == n_wide:
-            keep(sweep(start, LANES, kept()))
-
-    def near_cells(e):
-        for k in range(slots):
-            arrived(cell_in.at[0], cell_recv_sem, e * slots + k)
+            return on_bodies(near, total)
+        padded = jnp.concatenate([near, jnp.zeros((4, LANES), jnp.float32)], axis=0)
+        cols[pl.ds(pl.multiple_of(even * stars, LANES), LANES), :] = jnp.transpose(padded)
+        return total
+
+    def near_cells(e, total):
         parts = []
         for c in range(4):
             row = jnp.zeros((1, LANES), jnp.float32)
@@ -351,15 +399,18 @@
         for t in range(star_groups):
             for c, value in enumerate(cells_on_stars(rows, t)):
                 star_sum[t, c] = value
-        parts.append(jnp.zeros((4, LANES), jnp.float32))
-        start = pl.multiple_of(cell_at + e * LANES, LANES)
-        cols[pl.ds(start, LANES), :] = jnp.transpose(jnp.concatenate(parts, axis=0))
-        keep(sweep(start, LANES, kept()))
-
-    def all_stars(even):
+        return on_bodies(jnp.concatenate(parts, axis=0), total)
+
+    def near_arrived(even):
+        for w in (even, even + 1):
+            arrived(states.at[0, 0], near_sem, w)
+
+    def rest_arrived(even):
         for w in (even, even + 1):
             few = states.at[pl.ds(0, n_narrow - 1), 0]
             pltpu.make_async_copy(few, few, pass_recv_sem.at[w]).wait()
+
+    def all_stars(even):
         for n in range(n_narrow):
             rows, speeds = gather(n, even)
             srow[n, 0:4, :] = rows
@@ -400,35 +451,51 @@
             answer,
         )
         q = jnp.where(lower, p, halves - 1 - p)
-        near_stars(2 * q)
-
-        @pl.when(lax.rem(p, pairs_per_row) == pairs_per_row - 1)
-        def _():
-            near_cells(q // pairs_per_row)
-
-        all_stars(2 * q)
+        near_arrived(2 * q)
+        second = lax.rem(p, pairs_per_row) == pairs_per_row - 1
+
+        @pl.when(second)
+        def _():
+            e = q // pairs_per_row
+            for k in range(slots):
+                arrived(cell_in.at[0], cell_recv_sem, e * slots + k)
+            keep(near_cells(e, near_stars(2 * q, kept())))
+            rest_arrived(2 * q)
+            all_stars(2 * q)
+
+        @pl.when(jnp.logical_not(second))
+        def _():
+            rest_arrived(2 * q)
+            keep(near_stars(2 * q, kept()))
+            all_stars(2 * q)
 
     run(0, halves, turn)
 
     total = kept()
-    if kicks != n_wide:
-        kicked = []
-        for t in every:
-
-            def one_block(k, acc):
+    for t in every:
+        tile = slice(t * LANES, (t + 1) * LANES)
+        near = [gpos[c : c + 1, tile] for c in range(3)]
+        pieces = [jnp.sum(part, axis=0, keepdims=True) for part in total[t]]
+        pieces = [pieces[c] - near[c] * pieces[3] for c in range(3)]
+        if kicks != n_wide:
+            here = [spread(row) for row in near]
+
+            def kick(k, acc):
                 listed = star_leaf[t * leaves // tiles, k]
-                start = star_at + listed * stars
-                return loop(
-                    stars // ROWS, lambda g, part: on_bodies(start + g * ROWS, (t,), part), acc
-                )
-
-            kicked.append(lax.fori_loop(0, kicks, one_block, (total[t],))[0])
-        total = tuple(kicked)
-    for t in every:
+
+                def some(g, acc):
+                    at = pl.multiple_of(listed * stars + g * ROWS, ROWS)
+                    source = cols[pl.ds(at, ROWS), :]
+                    place = [column(source, c) for c in range(3)]
+                    return pull(place, column(source, 3), here, acc)
+
+                return loop(stars // ROWS, some, acc)
+
+            kicked = lax.fori_loop(0, kicks, kick, (zero,) * 3)
+            for c in range(3):
+                pieces[c] = pieces[c] + jnp.sum(kicked[c], axis=0, keepdims=True)
         for c in range(3):
-            piece = jnp.sum(total[t][c], axis=0, keepdims=True)
-            spot = (slice(c, c + 1), slice(t * LANES, (t + 1) * LANES))
-            out[spot] = gal_vel[spot] + time_step * piece
+            out[c : c + 1, tile] = gal_vel[c : c + 1, tile] + time_step * pieces[c]
 
     pieces = []
     for t in range(star_groups):
@@ -503,12 +570,14 @@
             pltpu.SMEM(star_leaf.shape, i32),
             pltpu.SemaphoreType.DMA((11,)),
             pltpu.VMEM((n_narrow, n_wide, 4, LANES), f32),
+            pltpu.VMEM((ROWS, LANES), f32),
             pltpu.VMEM((n_wide, 1, LANES), f32),
             pltpu.VMEM((n_wide, 1, LANES), f32),
-            pltpu.VMEM((bodies + n_wide * (stars + GROUPS), ROWS), f32),
+            pltpu.VMEM((32, bodies), jnp.bfloat16),
+            pltpu.VMEM((n_wide * stars, ROWS), f32),
             pltpu.VMEM((n_narrow, ROWS, LANES), f32),
             pltpu.VMEM((stars // ROWS, 6, ROWS, LANES), f32),
-            pltpu.VMEM((3 * bodies // LANES, ROWS, LANES), f32),
+            pltpu.VMEM((4 * bodies // LANES, ROWS, LANES), f32),
             pltpu.VMEM((stars // ROWS, 6, ROWS, LANES), f32),
             pltpu.SemaphoreType.DMA,
             pltpu.SemaphoreType.DMA((n_wide,)),

time: 12.5 us -> 12.2 us (0.976)
  the two profiles are of different devices: /device:TPU:0 before, /device:TPU:25 now
where the time goes in v3:
time: 12.2 us; the launch traced here: 12 us
  Pallas kernels  11.4 us (93%)
  between operations  0.64 us (5%)
    pallas_call x1, Pallas kernels, body(): pl.pallas_call(functools.partial(kernel, n_wide, n_narrow), out_shape=jax...  10.8 us
    pallas_call x1, Pallas kernels, body(): pl.pallas_call(unpack, out_shape=(jax.ShapeDtypeStruct(gal_vel.shape, f32...  0.61 us

profile of v3, /device:TPU:25, one launch (start us, length us, event | category | flops | bytes accessed | tf_op | source)
XLA Modules:
  0.0 12.0 jit_solution(9480057589098950200)
XLA Ops:
  0.6 10.8 %shard_map.130.packed = f32[3,768]{1,0:T(4,128)S(1)} custom-call(f32[3,64]{1,0:T(4,128)} %star_pos_hbm.1, f32[3,64]{1,0:T(4,128)} %star_vel_hbm.1, f32[1,64]{1,0:T(1,128)} %bitcast.6, f32[3,64]{1,0:T(4,128)} %star_acc_hbm.1, f32[3,64]{1,0:T(4,128)} %star_jerk_hbm.1, f32[3,512]{1,0:T(4,128)} %gal_pos_hbm.1, f32[3,512]{1,0:T(4,128)} %gal_vel_hbm.1, ...), custom_call_target="tpu_custom_call" | custom-call | tf_op jit(solution)/shard_map/pallas_call | solution.py:554
  11.4 0.6 %shard_map.131 = (f32[3,512]{1,0:T(4,128)}, f32[3,64]{1,0:T(4,128)}, f32[3,64]{1,0:T(4,128)}) custom-call(f32[3,768]{1,0:T(4,128)S(1)} %shard_map.130.packed), custom_call_target="tpu_custom_call" | custom-call | tf_op jit(solution)/shard_map/pallas_call | solution.py:611

commit v4 on v3

--- a/solution.py
+++ b/solution.py
@@ -201,8 +201,6 @@
         def _():
             pl.semaphore_wait(barrier, smaller)
 
-        run(0, wide, lambda w: signal_group(enter_sem.at[wide], w))
-        run(0, narrow, lambda n: signal(enter_sem.at[wide], wide, n))
 
         def send_down(w):
             send_group(w)
@@ -211,7 +209,11 @@
             def _():
                 send_cells(w)
 
-        run(0, wide, send_down)
+        one = jnp.minimum(wide, 1)
+        run(0, one, send_down)
+        run(0, wide, lambda w: signal_group(enter_sem.at[wide], w))
+        run(0, narrow, lambda n: signal(enter_sem.at[wide], wide, n))
+        run(one, wide, send_down)
         run(0, narrow, send_beside)
 
     def make_cells():
@@ -410,7 +412,7 @@
             few = states.at[pl.ds(0, n_narrow - 1), 0]
             pltpu.make_async_copy(few, few, pass_recv_sem.at[w]).wait()
 
-    def all_stars(even):
+    def all_stars(even, take):
         for n in range(n_narrow):
             rows, speeds = gather(n, even)
             srow[n, 0:4, :] = rows
@@ -437,17 +439,26 @@
                     acc[4] + (uy - dy * approach) * weight,
                     acc[5] + (uz - dz * approach) * weight,
                 ]
-            for c in range(6):
-                star_sum[t, c] = acc[c]
+            take(t, acc)
+
+    def store(t, acc):
+        for c in range(6):
+            star_sum[t, c] = acc[c]
 
     pairs_per_row = slots // 2
 
-    early = jnp.where(lower, halves, n_wide)
+    def nearby(q):
+        e = q // pairs_per_row
+        for k in range(slots):
+            arrived(cell_in.at[0], cell_recv_sem, e * slots + k)
+        return near_cells(e, near_stars(2 * q, kept()))
+
+    first = wide < n_wide // 8
 
     def turn(p):
         run(
-            jnp.where(p == 0, wide, early),
-            jnp.where(p == 0, early, jnp.where(p == 1, n_wide, 0)),
+            jnp.where(p == 0, wide, jnp.where(first, 2 * p + 2, n_wide)),
+            jnp.where(first, jnp.minimum(2 * p + 4, n_wide), n_wide),
             answer,
         )
         q = jnp.where(lower, p, halves - 1 - p)
@@ -456,22 +467,21 @@
 
         @pl.when(second)
         def _():
-            e = q // pairs_per_row
-            for k in range(slots):
-                arrived(cell_in.at[0], cell_recv_sem, e * slots + k)
-            keep(near_cells(e, near_stars(2 * q, kept())))
+            keep(nearby(q))
             rest_arrived(2 * q)
-            all_stars(2 * q)
+            all_stars(2 * q, store)
 
         @pl.when(jnp.logical_not(second))
         def _():
             rest_arrived(2 * q)
             keep(near_stars(2 * q, kept()))
-            all_stars(2 * q)
-
-    run(0, halves, turn)
-
-    total = kept()
+            all_stars(2 * q, store)
+
+    run(0, halves - 1, turn)
+
+    last = 2 * jnp.where(lower, halves - 1, 0)
+    near_arrived(last)
+    total = nearby(last // 2)
     for t in every:
         tile = slice(t * LANES, (t + 1) * LANES)
         near = [gpos[c : c + 1, tile] for c in range(3)]
@@ -498,13 +508,15 @@
             out[c : c + 1, tile] = gal_vel[c : c + 1, tile] + time_step * pieces[c]
 
     pieces = []
-    for t in range(star_groups):
+
+    def finish(t, acc):
         piece = jnp.zeros((ROWS, LANES), jnp.float32)
         for c in range(6):
-            piece = jnp.where(
-                lane8 == c, jnp.sum(star_sum[t, c], axis=1, keepdims=True), piece
-            )
+            piece = jnp.where(lane8 == c, jnp.sum(acc[c], axis=1, keepdims=True), piece)
         pieces.append(piece)
+
+    rest_arrived(last)
+    all_stars(last, finish)
     result = jnp.transpose(jnp.concatenate(pieces, axis=0))
     new_acc, new_jerk = result[0:3], result[3:6]
     vel_new = (

time: 12.2 us -> 12.2 us (level)
  no operation moved by 1% of the time
where the time goes in v4:
time: 12.2 us; the launch traced here: 12 us
  Pallas kernels  11.4 us (93%)
  between operations  0.64 us (5%)
    pallas_call x1, Pallas kernels, body(): pl.pallas_call(functools.partial(kernel, n_wide, n_narrow), out_shape=jax...  10.8 us
    pallas_call x1, Pallas kernels, body(): pl.pallas_call(unpack, out_shape=(jax.ShapeDtypeStruct(gal_vel.shape, f32...  0.61 us

profile of v4, /device:TPU:25, one launch (start us, length us, event | category | flops | bytes accessed | tf_op | source)
XLA Modules:
  0.0 12.0 jit_solution(11859858504347787852)
XLA Ops:
  0.6 10.8 %shard_map.130.packed = f32[3,768]{1,0:T(4,128)S(1)} custom-call(f32[3,64]{1,0:T(4,128)} %star_pos_hbm.1, f32[3,64]{1,0:T(4,128)} %star_vel_hbm.1, f32[1,64]{1,0:T(1,128)} %bitcast.6, f32[3,64]{1,0:T(4,128)} %star_acc_hbm.1, f32[3,64]{1,0:T(4,128)} %star_jerk_hbm.1, f32[3,512]{1,0:T(4,128)} %gal_pos_hbm.1, f32[3,512]{1,0:T(4,128)} %gal_vel_hbm.1, ...), custom_call_target="tpu_custom_call" | custom-call | tf_op jit(solution)/shard_map/pallas_call | solution.py:566
  11.4 0.6 %shard_map.131 = (f32[3,512]{1,0:T(4,128)}, f32[3,64]{1,0:T(4,128)}, f32[3,64]{1,0:T(4,128)}) custom-call(f32[3,768]{1,0:T(4,128)S(1)} %shard_map.130.packed), custom_call_target="tpu_custom_call" | custom-call | tf_op jit(solution)/shard_map/pallas_call | solution.py:623

commit v5 on v4

--- a/solution.py
+++ b/solution.py
@@ -63,14 +63,10 @@
     let_send_hbm,
     star_leaf_hbm,
     out,
-    star_pos,
-    star_vel,
+    star_in,
     star_mass,
-    star_acc,
-    star_jerk,
-    gal_pos,
-    gal_vel,
-    gal_mass,
+    gal_in,
+    masses,
     group_of,
     let_send,
     star_leaf,
@@ -87,15 +83,13 @@
     star_sum,
     send_sem,
     near_sem,
+    pass_sem,
     cell_send_sem,
     cell_recv_sem,
-    pass_send_sem,
-    pass_recv_sem,
     enter_sem,
 ):
     wide, narrow = lax.axis_index("wide"), lax.axis_index("narrow")
-    stars = star_pos.shape[1]
-    bodies = gal_pos.shape[1]
+    stars, bodies = star_in.shape[2], gal_in.shape[2]
     leaves, kicks = star_leaf.shape
     slots = LANES // GROUPS
     step_sq = time_step * time_step
@@ -103,25 +97,25 @@
     every = tuple(range(tiles))
 
     fetches = [
-        pltpu.make_async_copy(source, target, in_sem.at[i])
-        for i, (source, target) in enumerate(
-            (
-                (star_pos_hbm, star_pos),
-                (star_vel_hbm, star_vel),
-                (star_mass_hbm, star_mass),
-                (star_acc_hbm, star_acc),
-                (star_jerk_hbm, star_jerk),
-                (gal_pos_hbm, gal_pos),
-                (gal_vel_hbm, gal_vel),
-                (gal_mass_hbm, gal_mass),
-                (group_of_hbm, group_of),
-                (let_send_hbm, let_send),
-                (star_leaf_hbm, star_leaf),
-            )
-        )
+        (star_pos_hbm, star_in.at[0], 0),
+        (star_vel_hbm, star_in.at[1], 0),
+        (star_acc_hbm, star_in.at[2], 0),
+        (star_jerk_hbm, star_in.at[3], 0),
+        (star_mass_hbm, star_mass, 1),
+        (gal_pos_hbm, gal_in.at[0], 2),
+        (gal_vel_hbm, gal_in.at[1], 2),
+        (gal_mass_hbm, masses.at[0], 3),
+        (group_of_hbm, group_of, 3),
+        (let_send_hbm, let_send, 4),
     ]
-    for fetch in fetches:
-        fetch.start()
+    if kicks != n_wide:
+        fetches.append((star_leaf_hbm, star_leaf, 5))
+    for source, target, i in fetches:
+        pltpu.make_async_copy(source, target, in_sem.at[i]).start()
+
+    def fetched(*refs):
+        for ref, i in refs:
+            pltpu.make_async_copy(ref, ref, in_sem.at[i]).wait()
 
     barrier = pltpu.get_barrier_semaphore()
     others = [lax.rem(narrow + m, n_narrow) for m in range(1, n_narrow)]
@@ -149,11 +143,8 @@
     row8 = lax.broadcasted_iota(jnp.int32, (ROWS, LANES), 0)
     left = lane4 < stars
 
-    for fetch in fetches[:5]:
-        fetch.wait()
-
-    spos, svel = star_pos[...], star_vel[...]
-    sacc, sjerk = star_acc[...], star_jerk[...]
+    fetched((star_in, 0), (star_mass, 1))
+    spos, svel, sacc, sjerk = (star_in[i] for i in range(4))
     pred_pos = (
         spos + time_step * svel + step_sq * 0.5 * sacc + step_sq * time_step / 6.0 * sjerk
     )
@@ -162,32 +153,33 @@
     vel4 = jnp.concatenate([pred_vel, jnp.zeros((1, stars), jnp.float32)], axis=0)
     block = jnp.concatenate([pos4, vel4], axis=1)
     block = jnp.where(lax.rem(wide, 2) == 0, block, pltpu.roll(block, stars, 1))
-    states[narrow, wide] = block
-
-    def send_state(w, n, sends, recvs):
+    mine = narrow * n_wide + wide
+    states[mine] = block
+
+    def send_state(w, n, recvs):
         pltpu.make_async_remote_copy(
-            src_ref=states.at[narrow, wide],
-            dst_ref=states.at[narrow, wide],
-            send_sem=sends,
-            recv_sem=recvs.at[wide],
+            src_ref=states.at[mine],
+            dst_ref=states.at[mine],
+            send_sem=send_sem,
+            recv_sem=recvs.at[wide // 2],
             device_id=(w, n),
             device_id_type=MESH,
         ).start()
 
     def send_group(w):
-        send_state(w, narrow, send_sem, near_sem)
+        send_state(w, narrow, near_sem)
         for n in others:
-            send_state(w, n, pass_send_sem, pass_recv_sem)
+            send_state(w, n, pass_sem)
 
     def send_beside(n):
-        send_state(wide, n, pass_send_sem, pass_recv_sem)
+        send_state(wide, n, pass_sem)
 
     def send_cells(w):
         pltpu.make_async_remote_copy(
             src_ref=cell_out.at[w],
             dst_ref=cell_in.at[wide],
             send_sem=cell_send_sem,
-            recv_sem=cell_recv_sem.at[wide],
+            recv_sem=cell_recv_sem.at[wide // slots],
             device_id=(w, narrow),
             device_id_type=MESH,
         ).start()
@@ -201,7 +193,6 @@
         def _():
             pl.semaphore_wait(barrier, smaller)
 
-
         def send_down(w):
             send_group(w)
 
@@ -211,15 +202,16 @@
 
         one = jnp.minimum(wide, 1)
         run(0, one, send_down)
-        run(0, wide, lambda w: signal_group(enter_sem.at[wide], w))
-        run(0, narrow, lambda n: signal(enter_sem.at[wide], wide, n))
+        run(0, wide, lambda w: signal_group(enter_sem.at[wide // 2], w))
+        run(0, narrow, lambda n: signal(enter_sem.at[wide // 2], wide, n))
         run(one, wide, send_down)
         run(0, narrow, send_beside)
 
     def make_cells():
-        for fetch in fetches[5:]:
-            fetch.wait()
-        gpos, gmass = gal_pos[...], gal_mass[...]
+        fetched((gal_in, 2), (masses, 3), (let_send, 4))
+        if kicks != n_wide:
+            fetched((star_leaf, 5))
+        gpos, gmass = gal_in[0], masses[0]
         body_lane = lax.broadcasted_iota(jnp.int32, (1, bodies), 1)
         segment = group_of[...] + (body_lane // (bodies // leaves)) * GROUPS
         onehot = (
@@ -279,7 +271,7 @@
     def _():
         run(0, wide, send_cells)
 
-    gpos, gmass = gal_pos[...], gal_mass[...]
+    gpos, gmass = gal_in[0], masses[0]
 
     both = jnp.concatenate([pos4, vel4], axis=0)
     targets = jnp.transpose(
@@ -290,11 +282,11 @@
     own = [spread(cell_own[c : c + 1, :]) for c in range(4)]
     star_groups = stars // ROWS
     for t in range(star_groups):
-        mine = targets[t * ROWS : (t + 1) * ROWS, :]
-        place = [column(mine, c) for c in range(3)]
+        rows = targets[t * ROWS : (t + 1) * ROWS, :]
+        place = [column(rows, c) for c in range(3)]
         for c in range(3):
             aims[t, c] = place[c]
-            aims[t, 3 + c] = column(mine, 4 + c)
+            aims[t, 3 + c] = column(rows, 4 + c)
             star_sum[t, 3 + c] = zero
         for c, value in enumerate(pull(own[:3], own[3], place, (zero,) * 3)):
             star_sum[t, c] = value
@@ -321,9 +313,9 @@
         )
         total = [list(part) for part in total]
         for g in range(LANES // ROWS):
-            mine = turned[g * ROWS : (g + 1) * ROWS, :]
-            place = [column(mine, 28 + c) for c in range(3)]
-            mass = column(mine, 31)
+            some = turned[g * ROWS : (g + 1) * ROWS, :]
+            place = [column(some, 28 + c) for c in range(3)]
+            mass = column(some, 31)
             for t in every:
                 inverse = lax.rsqrt(
                     reach[g * ROWS : (g + 1) * ROWS, t * LANES : (t + 1) * LANES]
@@ -352,35 +344,53 @@
         total = on_bodies(jnp.concatenate([gpos[:, tile], gmass[:, tile]], axis=0), total)
     keep(total)
 
-    def answer(w):
-        @pl.when(w == wide)
-        def _():
-            @pl.when(narrow < n_narrow - 1)
+    def larger(w):
+        rest = jnp.where(w == wide, n_narrow - 1 - narrow, 0)
+        return jnp.where(w > wide, n_narrow, rest)
+
+    def answer(q):
+        count = larger(2 * q) + larger(2 * q + 1)
+
+        @pl.when(count > 0)
+        def _():
+            pl.semaphore_wait(enter_sem.at[q], count)
+
+        def to_group(w):
+            @pl.when(w == wide)
             def _():
-                pl.semaphore_wait(enter_sem.at[wide], n_narrow - 1 - narrow)
-
-            run(narrow + 1, n_narrow, send_beside)
-
-        @pl.when(w > wide)
-        def _():
-            pl.semaphore_wait(enter_sem.at[w], n_narrow)
-            send_group(w)
-            send_cells(w)
+                run(narrow + 1, n_narrow, send_beside)
+
+            @pl.when(w > wide)
+            def _():
+                send_group(w)
+                send_cells(w)
+
+        run(2 * q, 2 * q + 2, to_group)
 
     halves = n_wide // 2
     lower = wide < n_wide // 4
 
 
     def gather(n, even):
-        even_block, odd_block = states[n, even], states[n, even + 1]
+        even_block, odd_block = states[n * n_wide + even], states[n * n_wide + even + 1]
         rows = jnp.where(left, even_block, odd_block)
         speeds = pltpu.roll(jnp.where(left, odd_block, even_block), stars, 1)
         return rows, speeds
 
-    def arrived(ref, sem, w):
-        @pl.when(w != wide)
-        def _():
-            pltpu.make_async_copy(ref, ref, sem.at[w]).wait()
+    def arrived(ref, size, sem, i):
+        own = wide // size == i
+
+        def wait(count):
+            some = ref.at[pl.ds(0, count)]
+            pltpu.make_async_copy(some, some, sem.at[i]).wait()
+
+        @pl.when(own)
+        def _():
+            wait(size - 1)
+
+        @pl.when(jnp.logical_not(own))
+        def _():
+            wait(size)
 
     def near_stars(even, total):
         near, _ = gather(narrow, even)
@@ -403,14 +413,9 @@
                 star_sum[t, c] = value
         return on_bodies(jnp.concatenate(parts, axis=0), total)
 
-    def near_arrived(even):
-        for w in (even, even + 1):
-            arrived(states.at[0, 0], near_sem, w)
-
-    def rest_arrived(even):
-        for w in (even, even + 1):
-            few = states.at[pl.ds(0, n_narrow - 1), 0]
-            pltpu.make_async_copy(few, few, pass_recv_sem.at[w]).wait()
+    def rest_arrived(q):
+        some = states.at[pl.ds(0, 2 * (n_narrow - 1))]
+        pltpu.make_async_copy(some, some, pass_sem.at[q]).wait()
 
     def all_stars(even, take):
         for n in range(n_narrow):
@@ -449,39 +454,38 @@
 
     def nearby(q):
         e = q // pairs_per_row
-        for k in range(slots):
-            arrived(cell_in.at[0], cell_recv_sem, e * slots + k)
+        arrived(cell_in, slots, cell_recv_sem, e)
         return near_cells(e, near_stars(2 * q, kept()))
 
     first = wide < n_wide // 8
 
     def turn(p):
         run(
-            jnp.where(p == 0, wide, jnp.where(first, 2 * p + 2, n_wide)),
-            jnp.where(first, jnp.minimum(2 * p + 4, n_wide), n_wide),
+            jnp.where(p == 0, wide // 2, jnp.where(first, p + 1, halves)),
+            jnp.where(first, jnp.minimum(p + 2, halves), halves),
             answer,
         )
         q = jnp.where(lower, p, halves - 1 - p)
-        near_arrived(2 * q)
+        arrived(states, 2, near_sem, q)
         second = lax.rem(p, pairs_per_row) == pairs_per_row - 1
 
         @pl.when(second)
         def _():
             keep(nearby(q))
-            rest_arrived(2 * q)
+            rest_arrived(q)
             all_stars(2 * q, store)
 
         @pl.when(jnp.logical_not(second))
         def _():
-            rest_arrived(2 * q)
+            rest_arrived(q)
             keep(near_stars(2 * q, kept()))
             all_stars(2 * q, store)
 
     run(0, halves - 1, turn)
 
-    last = 2 * jnp.where(lower, halves - 1, 0)
-    near_arrived(last)
-    total = nearby(last // 2)
+    last = jnp.where(lower, halves - 1, 0)
+    arrived(states, 2, near_sem, last)
+    total = nearby(last)
     for t in every:
         tile = slice(t * LANES, (t + 1) * LANES)
         near = [gpos[c : c + 1, tile] for c in range(3)]
@@ -505,7 +509,7 @@
             for c in range(3):
                 pieces[c] = pieces[c] + jnp.sum(kicked[c], axis=0, keepdims=True)
         for c in range(3):
-            out[c : c + 1, tile] = gal_vel[c : c + 1, tile] + time_step * pieces[c]
+            out[c : c + 1, tile] = gal_in[1, c : c + 1, tile] + time_step * pieces[c]
 
     pieces = []
 
@@ -516,7 +520,7 @@
         pieces.append(piece)
 
     rest_arrived(last)
-    all_stars(last, finish)
+    all_stars(2 * last, finish)
     result = jnp.transpose(jnp.concatenate(pieces, axis=0))
     new_acc, new_jerk = result[0:3], result[3:6]
     vel_new = (
@@ -528,12 +532,10 @@
         spos + time_step * 0.5 * (svel + vel_new) + step_sq / 12.0 * (sacc - new_acc)
     )
 
-    some = states.at[0, pl.ds(0, n_wide - 1)]
+    some = states.at[pl.ds(0, n_wide * n_narrow - 1)]
+    pltpu.make_async_copy(some, some, send_sem).wait()
     few = cell_in.at[pl.ds(0, n_wide - 1)]
-    rest = states.at[pl.ds(0, n_narrow - 1)]
-    pltpu.make_async_copy(some, some, send_sem).wait()
     pltpu.make_async_copy(few, few, cell_send_sem).wait()
-    pltpu.make_async_copy(rest, rest, pass_send_sem).wait()
 
 
 def unpack(packed, gal_out, pos_out, vel_out):
@@ -569,19 +571,15 @@
         in_specs=[hbm] * 11,
         out_specs=vmem,
         scratch_shapes=[
-            pltpu.VMEM((3, stars), f32),
-            pltpu.VMEM((3, stars), f32),
+            pltpu.VMEM((4, 3, stars), f32),
             pltpu.VMEM((1, stars), f32),
-            pltpu.VMEM((3, stars), f32),
-            pltpu.VMEM((3, stars), f32),
-            pltpu.VMEM((3, bodies), f32),
-            pltpu.VMEM((3, bodies), f32),
-            pltpu.VMEM((1, bodies), f32),
+            pltpu.VMEM((2, 3, bodies), f32),
+            pltpu.VMEM((2, 1, bodies), f32),
             pltpu.VMEM((1, bodies), i32),
             pltpu.VMEM((1, n_wide), i32),
             pltpu.SMEM(star_leaf.shape, i32),
-            pltpu.SemaphoreType.DMA((11,)),
-            pltpu.VMEM((n_narrow, n_wide, 4, LANES), f32),
+            pltpu.SemaphoreType.DMA((5 + (star_leaf.shape[1] != n_wide),)),
+            pltpu.VMEM((n_narrow * n_wide, 4, LANES), f32),
             pltpu.VMEM((ROWS, LANES), f32),
             pltpu.VMEM((n_wide, 1, LANES), f32),
             pltpu.VMEM((n_wide, 1, LANES), f32),
@@ -592,12 +590,11 @@
             pltpu.VMEM((4 * bodies // LANES, ROWS, LANES), f32),
             pltpu.VMEM((stars // ROWS, 6, ROWS, LANES), f32),
             pltpu.SemaphoreType.DMA,
-            pltpu.SemaphoreType.DMA((n_wide,)),
+            pltpu.SemaphoreType.DMA((n_wide // 2,)),
+            pltpu.SemaphoreType.DMA((n_wide // 2,)),
             pltpu.SemaphoreType.DMA,
-            pltpu.SemaphoreType.DMA((n_wide,)),
-            pltpu.SemaphoreType.DMA,
-            pltpu.SemaphoreType.DMA((n_wide,)),
-            pltpu.SemaphoreType.REGULAR((n_wide,)),
+            pltpu.SemaphoreType.DMA((n_wide * GROUPS // LANES,)),
+            pltpu.SemaphoreType.REGULAR((n_wide // 2,)),
         ],
         compiler_params=pltpu.CompilerParams(
             collective_id=0, has_side_effects=True, vmem_limit_bytes=24 << 20

time: 12.2 us -> 11.9 us (0.975)
  Pallas kernels: 11.4 us -> 11.1 us
    pallas_call x1, Pallas kernels: 10.8 us -> 10.5 us  [body(): pl.pallas_call(functools.partial(kernel, n_wide, n_narrow), out_shape=jax...]
where the time goes in v5:
time: 11.9 us; the launch traced here: 11.8 us
  Pallas kernels  11.1 us (93%)
  between operations  0.64 us (5%)
    pallas_call x1, Pallas kernels, body(): pl.pallas_call(functools.partial(kernel, n_wide, n_narrow), out_shape=jax...  10.5 us
    pallas_call x1, Pallas kernels, body(): pl.pallas_call(unpack, out_shape=(jax.ShapeDtypeStruct(gal_vel.shape, f32...  0.61 us

profile of v5, /device:TPU:25, one launch (start us, length us, event | category | flops | bytes accessed | tf_op | source)
XLA Modules:
  0.0 11.8 jit_solution(11274994519599024272)
XLA Ops:
  0.6 10.5 %shard_map.130.packed = f32[3,768]{1,0:T(4,128)S(1)} custom-call(f32[3,64]{1,0:T(4,128)} %star_pos_hbm.1, f32[3,64]{1,0:T(4,128)} %star_vel_hbm.1, f32[1,64]{1,0:T(1,128)} %bitcast.6, f32[3,64]{1,0:T(4,128)} %star_acc_hbm.1, f32[3,64]{1,0:T(4,128)} %star_jerk_hbm.1, f32[3,512]{1,0:T(4,128)} %gal_pos_hbm.1, f32[3,512]{1,0:T(4,128)} %gal_vel_hbm.1, ...), custom_call_target="tpu_custom_call" | custom-call | tf_op jit(solution)/shard_map/pallas_call | solution.py:568
  11.2 0.6 %shard_map.131 = (f32[3,512]{1,0:T(4,128)}, f32[3,64]{1,0:T(4,128)}, f32[3,64]{1,0:T(4,128)}) custom-call(f32[3,768]{1,0:T(4,128)S(1)} %shard_map.130.packed), custom_call_target="tpu_custom_call" | custom-call | tf_op jit(solution)/shard_map/pallas_call | solution.py:620

commit v6 on v5

--- a/solution.py
+++ b/solution.py
@@ -84,8 +84,6 @@
     send_sem,
     near_sem,
     pass_sem,
-    cell_send_sem,
-    cell_recv_sem,
     enter_sem,
 ):
     wide, narrow = lax.axis_index("wide"), lax.axis_index("narrow")
@@ -178,8 +176,8 @@
         pltpu.make_async_remote_copy(
             src_ref=cell_out.at[w],
             dst_ref=cell_in.at[wide],
-            send_sem=cell_send_sem,
-            recv_sem=cell_recv_sem.at[wide // slots],
+            send_sem=send_sem,
+            recv_sem=near_sem.at[wide // 2],
             device_id=(w, narrow),
             device_id_type=MESH,
         ).start()
@@ -231,7 +229,6 @@
         cells = jnp.where(row8 < 3, sums / spread(sums[3:4]), sums)
         cell_own[...] = cells
 
-        part = jnp.bitwise_and(group - lax.rem(wide, slots), slots - 1)
         square = (n_wide, n_wide)
         diagonal = lax.broadcasted_iota(jnp.int32, square, 0) == lax.broadcasted_iota(
             jnp.int32, square, 1
@@ -239,20 +236,19 @@
         listed = jnp.broadcast_to(let_send[...].astype(jnp.float32), square)
         chosen = jnp.sum(jnp.where(diagonal, listed, 0.0), axis=1, keepdims=True)
         chosen = jnp.broadcast_to(chosen, (n_wide, LANES)).astype(jnp.int32)
-        outgoing = jnp.zeros((n_wide, LANES), jnp.float32)
-        pick = jnp.bitwise_and(group - chosen, slots - 1)
-        for k in range(slots):
-            turned = cells if k == 0 else pltpu.roll(cells, k * GROUPS, 1)
-            base = jnp.zeros((1, LANES), jnp.float32)
-            for c in range(4):
-                base = jnp.where(part == c, turned[c : c + 1], base)
-            outgoing = jnp.where(
-                jnp.logical_and(pick == k, chosen >= 0),
-                jnp.broadcast_to(base, (n_wide, LANES)),
-                outgoing,
-            )
-        cell_out[:, 0, :] = outgoing
-        cell_in[wide] = jnp.zeros((1, LANES), jnp.float32)
+        place = lax.rem(wide, slots)
+        turn = jnp.bitwise_and(place - chosen, slots - 1)
+        turn = jnp.where(jnp.logical_and(group == place, chosen >= 0), turn, slots)
+        turned = [
+            (cells if k == 0 else pltpu.roll(cells, k * GROUPS, 1))[0:4] for k in range(slots)
+        ]
+        for w in range(n_wide):
+            taken = jnp.broadcast_to(turn[w : w + 1], (4, LANES))
+            outgoing = jnp.zeros((4, LANES), jnp.float32)
+            for k in range(slots):
+                outgoing = jnp.where(taken == k, turned[k], outgoing)
+            cell_out[w] = outgoing
+        cell_in[wide] = jnp.zeros((4, LANES), jnp.float32)
 
     cells_first = jnp.logical_or(lax.rem(wide, 2) == 0, narrow < n_narrow // 2)
 
@@ -377,20 +373,20 @@
         speeds = pltpu.roll(jnp.where(left, odd_block, even_block), stars, 1)
         return rows, speeds
 
-    def arrived(ref, size, sem, i):
-        own = wide // size == i
+    def near_arrived(q):
+        own = wide // 2 == q
 
         def wait(count):
-            some = ref.at[pl.ds(0, count)]
-            pltpu.make_async_copy(some, some, sem.at[i]).wait()
+            some = states.at[pl.ds(0, count)]
+            pltpu.make_async_copy(some, some, near_sem.at[q]).wait()
 
         @pl.when(own)
         def _():
-            wait(size - 1)
+            wait(2)
 
         @pl.when(jnp.logical_not(own))
         def _():
-            wait(size)
+            wait(4)
 
     def near_stars(even, total):
         near, _ = gather(narrow, even)
@@ -401,17 +397,14 @@
         return total
 
     def near_cells(e, total):
-        parts = []
-        for c in range(4):
-            row = jnp.zeros((1, LANES), jnp.float32)
-            for k in range(slots):
-                row = jnp.where(group == (c + k) % slots, cell_in[e * slots + k], row)
-            parts.append(row if c == 0 else pltpu.roll(row, LANES - c * GROUPS, 1))
-        rows = [spread(part) for part in parts]
+        cells = cell_in[e * slots]
+        for k in range(1, slots):
+            cells = cells + cell_in[e * slots + k]
+        rows = [spread(cells[c : c + 1]) for c in range(4)]
         for t in range(star_groups):
             for c, value in enumerate(cells_on_stars(rows, t)):
                 star_sum[t, c] = value
-        return on_bodies(jnp.concatenate(parts, axis=0), total)
+        return on_bodies(cells, total)
 
     def rest_arrived(q):
         some = states.at[pl.ds(0, 2 * (n_narrow - 1))]
@@ -453,9 +446,7 @@
     pairs_per_row = slots // 2
 
     def nearby(q):
-        e = q // pairs_per_row
-        arrived(cell_in, slots, cell_recv_sem, e)
-        return near_cells(e, near_stars(2 * q, kept()))
+        return near_cells(q // pairs_per_row, near_stars(2 * q, kept()))
 
     first = wide < n_wide // 8
 
@@ -466,7 +457,7 @@
             answer,
         )
         q = jnp.where(lower, p, halves - 1 - p)
-        arrived(states, 2, near_sem, q)
+        near_arrived(q)
         second = lax.rem(p, pairs_per_row) == pairs_per_row - 1
 
         @pl.when(second)
@@ -484,7 +475,7 @@
     run(0, halves - 1, turn)
 
     last = jnp.where(lower, halves - 1, 0)
-    arrived(states, 2, near_sem, last)
+    near_arrived(last)
     total = nearby(last)
     for t in every:
         tile = slice(t * LANES, (t + 1) * LANES)
@@ -532,10 +523,8 @@
         spos + time_step * 0.5 * (svel + vel_new) + step_sq / 12.0 * (sacc - new_acc)
     )
 
-    some = states.at[pl.ds(0, n_wide * n_narrow - 1)]
-    pltpu.make_async_copy(some, some, send_sem).wait()
-    few = cell_in.at[pl.ds(0, n_wide - 1)]
-    pltpu.make_async_copy(few, few, cell_send_sem).wait()
+    sent = states.at[pl.ds(0, n_wide * (n_narrow + 1) - 2)]
+    pltpu.make_async_copy(sent, sent, send_sem).wait()
 
 
 def unpack(packed, gal_out, pos_out, vel_out):
@@ -579,10 +568,10 @@
             pltpu.VMEM((1, n_wide), i32),
             pltpu.SMEM(star_leaf.shape, i32),
             pltpu.SemaphoreType.DMA((5 + (star_leaf.shape[1] != n_wide),)),
-            pltpu.VMEM((n_narrow * n_wide, 4, LANES), f32),
+            pltpu.VMEM(((n_narrow + 1) * n_wide, 4, LANES), f32),
             pltpu.VMEM((ROWS, LANES), f32),
-            pltpu.VMEM((n_wide, 1, LANES), f32),
-            pltpu.VMEM((n_wide, 1, LANES), f32),
+            pltpu.VMEM((n_wide, 4, LANES), f32),
+            pltpu.VMEM((n_wide, 4, LANES), f32),
             pltpu.VMEM((32, bodies), jnp.bfloat16),
             pltpu.VMEM((n_wide * stars, ROWS), f32),
             pltpu.VMEM((n_narrow, ROWS, LANES), f32),
@@ -592,8 +581,6 @@
             pltpu.SemaphoreType.DMA,
             pltpu.SemaphoreType.DMA((n_wide // 2,)),
             pltpu.SemaphoreType.DMA((n_wide // 2,)),
-            pltpu.SemaphoreType.DMA,
-            pltpu.SemaphoreType.DMA((n_wide * GROUPS // LANES,)),
             pltpu.SemaphoreType.REGULAR((n_wide // 2,)),
         ],
         compiler_params=pltpu.CompilerParams(

time: 11.9 us -> 11.9 us (level)
  no operation moved by 1% of the time
where the time goes in v6:
time: 11.9 us; the launch traced here: 11.7 us
  Pallas kernels  11.1 us (93%)
  between operations  0.64 us (5%)
    pallas_call x1, Pallas kernels, body(): pl.pallas_call(functools.partial(kernel, n_wide, n_narrow), out_shape=jax...  10.5 us
    pallas_call x1, Pallas kernels, body(): pl.pallas_call(unpack, out_shape=(jax.ShapeDtypeStruct(gal_vel.shape, f32...  0.61 us

profile of v6, /device:TPU:25, one launch (start us, length us, event | category | flops | bytes accessed | tf_op | source)
XLA Modules:
  0.0 11.7 jit_solution(13764859840693584893)
XLA Ops:
  0.6 10.5 %shard_map.130.packed = f32[3,768]{1,0:T(4,128)S(1)} custom-call(f32[3,64]{1,0:T(4,128)} %star_pos_hbm.1, f32[3,64]{1,0:T(4,128)} %star_vel_hbm.1, f32[1,64]{1,0:T(1,128)} %bitcast.6, f32[3,64]{1,0:T(4,128)} %star_acc_hbm.1, f32[3,64]{1,0:T(4,128)} %star_jerk_hbm.1, f32[3,512]{1,0:T(4,128)} %gal_pos_hbm.1, f32[3,512]{1,0:T(4,128)} %gal_vel_hbm.1, ...), custom_call_target="tpu_custom_call" | custom-call | tf_op jit(solution)/shard_map/pallas_call | solution.py:557
  11.1 0.6 %shard_map.131 = (f32[3,512]{1,0:T(4,128)}, f32[3,64]{1,0:T(4,128)}, f32[3,64]{1,0:T(4,128)}) custom-call(f32[3,768]{1,0:T(4,128)S(1)} %shard_map.130.packed), custom_call_target="tpu_custom_call" | custom-call | tf_op jit(solution)/shard_map/pallas_call | solution.py:607

commit v7 on v6

--- a/solution.py
+++ b/solution.py
@@ -116,7 +116,8 @@
             pltpu.make_async_copy(ref, ref, in_sem.at[i]).wait()
 
     barrier = pltpu.get_barrier_semaphore()
-    others = [lax.rem(narrow + m, n_narrow) for m in range(1, n_narrow)]
+    half = n_narrow // 2
+    others = [lax.rem(narrow + half + m, n_narrow) for m in range(n_narrow) if m != half]
 
     def run(first, last, step):
         def body(i, carry):
@@ -169,6 +170,11 @@
         for n in others:
             send_state(w, n, pass_sem)
 
+    def answer_group(w):
+        for n in others:
+            send_state(w, n, pass_sem)
+        send_state(w, narrow, near_sem)
+
     def send_beside(n):
         send_state(wide, n, pass_sem)
 
@@ -198,7 +204,7 @@
             def _():
                 send_cells(w)
 
-        one = jnp.minimum(wide, 1)
+        one = jnp.where(lax.rem(wide, 2) == 0, 0, jnp.minimum(wide, 1))
         run(0, one, send_down)
         run(0, wide, lambda w: signal_group(enter_sem.at[wide // 2], w))
         run(0, narrow, lambda n: signal(enter_sem.at[wide // 2], wide, n))
@@ -358,7 +364,7 @@
 
             @pl.when(w > wide)
             def _():
-                send_group(w)
+                answer_group(w)
                 send_cells(w)
 
         run(2 * q, 2 * q + 2, to_group)
@@ -452,8 +458,8 @@
 
     def turn(p):
         run(
-            jnp.where(p == 0, wide // 2, jnp.where(first, p + 1, halves)),
-            jnp.where(first, jnp.minimum(p + 2, halves), halves),
+            jnp.where(p == 0, wide // 2, jnp.where(jnp.logical_and(first, p == 1), 2, halves)),
+            jnp.where(jnp.logical_and(first, p == 0), 2, halves),
             answer,
         )
         q = jnp.where(lower, p, halves - 1 - p)

time: 11.9 us -> 11.8 us (level)
  no operation moved by 1% of the time
where the time goes in v7:
time: 11.8 us; the launch traced here: 11.7 us
  Pallas kernels  11 us (93%)
  between operations  0.64 us (5%)
    pallas_call x1, Pallas kernels, body(): pl.pallas_call(functools.partial(kernel, n_wide, n_narrow), out_shape=jax...  10.4 us
    pallas_call x1, Pallas kernels, body(): pl.pallas_call(unpack, out_shape=(jax.ShapeDtypeStruct(gal_vel.shape, f32...  0.61 us

profile of v7, /device:TPU:25, one launch (start us, length us, event | category | flops | bytes accessed | tf_op | source)
XLA Modules:
  0.0 11.7 jit_solution(10072325705982925643)
XLA Ops:
  0.6 10.4 %shard_map.130.packed = f32[3,768]{1,0:T(4,128)S(1)} custom-call(f32[3,64]{1,0:T(4,128)} %star_pos_hbm.1, f32[3,64]{1,0:T(4,128)} %star_vel_hbm.1, f32[1,64]{1,0:T(1,128)} %bitcast.6, f32[3,64]{1,0:T(4,128)} %star_acc_hbm.1, f32[3,64]{1,0:T(4,128)} %star_jerk_hbm.1, f32[3,512]{1,0:T(4,128)} %gal_pos_hbm.1, f32[3,512]{1,0:T(4,128)} %gal_vel_hbm.1, ...), custom_call_target="tpu_custom_call" | custom-call | tf_op jit(solution)/shard_map/pallas_call | solution.py:563
  11.1 0.6 %shard_map.131 = (f32[3,512]{1,0:T(4,128)}, f32[3,64]{1,0:T(4,128)}, f32[3,64]{1,0:T(4,128)}) custom-call(f32[3,768]{1,0:T(4,128)S(1)} %shard_map.130.packed), custom_call_target="tpu_custom_call" | custom-call | tf_op jit(solution)/shard_map/pallas_call | solution.py:613

commit v8 on v7

--- a/solution.py
+++ b/solution.py
@@ -306,7 +306,7 @@
     def on_bodies(rows, total):
         square = norm(rows[0:3])
         high, mid, low = split(jnp.concatenate([rows[0:3], square], axis=0))
-        ones = jnp.ones((4, LANES), jnp.float32)
+        ones = jnp.ones(rows.shape, jnp.float32)
         turned = jnp.transpose(
             jnp.concatenate([high, high, mid, high, low, mid, ones, rows], axis=0)
         )
@@ -314,7 +314,7 @@
             turned.astype(jnp.bfloat16), aimed[...], preferred_element_type=jnp.float32
         )
         total = [list(part) for part in total]
-        for g in range(LANES // ROWS):
+        for g in range(rows.shape[1] // ROWS):
             some = turned[g * ROWS : (g + 1) * ROWS, :]
             place = [column(some, 28 + c) for c in range(3)]
             mass = column(some, 31)
@@ -394,15 +394,15 @@
         def _():
             wait(4)
 
-    def near_stars(even, total):
+    def near_stars(even):
         near, _ = gather(narrow, even)
         if kicks == n_wide:
-            return on_bodies(near, total)
+            return [near]
         padded = jnp.concatenate([near, jnp.zeros((4, LANES), jnp.float32)], axis=0)
         cols[pl.ds(pl.multiple_of(even * stars, LANES), LANES), :] = jnp.transpose(padded)
-        return total
-
-    def near_cells(e, total):
+        return []
+
+    def near_cells(e):
         cells = cell_in[e * slots]
         for k in range(1, slots):
             cells = cells + cell_in[e * slots + k]
@@ -410,7 +410,7 @@
         for t in range(star_groups):
             for c, value in enumerate(cells_on_stars(rows, t)):
                 star_sum[t, c] = value
-        return on_bodies(cells, total)
+        return [cells]
 
     def rest_arrived(q):
         some = states.at[pl.ds(0, 2 * (n_narrow - 1))]
@@ -452,7 +452,8 @@
     pairs_per_row = slots // 2
 
     def nearby(q):
-        return near_cells(q // pairs_per_row, near_stars(2 * q, kept()))
+        near = near_stars(2 * q) + near_cells(q // pairs_per_row)
+        return on_bodies(jnp.concatenate(near, axis=1), kept())
 
     first = wide < n_wide // 8
 
@@ -475,7 +476,8 @@
         @pl.when(jnp.logical_not(second))
         def _():
             rest_arrived(q)
-            keep(near_stars(2 * q, kept()))
+            for rows in near_stars(2 * q):
+                keep(on_bodies(rows, kept()))
             all_stars(2 * q, store)
 
     run(0, halves - 1, turn)

time: 11.8 us -> 11.8 us (level)
  no operation moved by 1% of the time
where the time goes in v8:
time: 11.8 us; the launch traced here: 11.6 us
  Pallas kernels  11 us (93%)
  between operations  0.64 us (5%)
    pallas_call x1, Pallas kernels, body(): pl.pallas_call(functools.partial(kernel, n_wide, n_narrow), out_shape=jax...  10.4 us
    pallas_call x1, Pallas kernels, body(): pl.pallas_call(unpack, out_shape=(jax.ShapeDtypeStruct(gal_vel.shape, f32...  0.61 us

profile of v8, /device:TPU:25, one launch (start us, length us, event | category | flops | bytes accessed | tf_op | source)
XLA Modules:
  0.0 11.6 jit_solution(9497951027502593170)
XLA Ops:
  0.6 10.4 %shard_map.130.packed = f32[3,768]{1,0:T(4,128)S(1)} custom-call(f32[3,64]{1,0:T(4,128)} %star_pos_hbm.1, f32[3,64]{1,0:T(4,128)} %star_vel_hbm.1, f32[1,64]{1,0:T(1,128)} %bitcast.6, f32[3,64]{1,0:T(4,128)} %star_acc_hbm.1, f32[3,64]{1,0:T(4,128)} %star_jerk_hbm.1, f32[3,512]{1,0:T(4,128)} %gal_pos_hbm.1, f32[3,512]{1,0:T(4,128)} %gal_vel_hbm.1, ...), custom_call_target="tpu_custom_call" | custom-call | tf_op jit(solution)/shard_map/pallas_call | solution.py:565
  11.0 0.6 %shard_map.131 = (f32[3,512]{1,0:T(4,128)}, f32[3,64]{1,0:T(4,128)}, f32[3,64]{1,0:T(4,128)}) custom-call(f32[3,768]{1,0:T(4,128)S(1)} %shard_map.130.packed), custom_call_target="tpu_custom_call" | custom-call | tf_op jit(solution)/shard_map/pallas_call | solution.py:615

commit v9 on v8

--- a/solution.py
+++ b/solution.py
@@ -469,8 +469,8 @@
 
         @pl.when(second)
         def _():
+            rest_arrived(q)
             keep(nearby(q))
-            rest_arrived(q)
             all_stars(2 * q, store)
 
         @pl.when(jnp.logical_not(second))
@@ -518,6 +518,8 @@
             piece = jnp.where(lane8 == c, jnp.sum(acc[c], axis=1, keepdims=True), piece)
         pieces.append(piece)
 
+    sent = states.at[pl.ds(0, n_wide * (n_narrow + 1) - 2)]
+    pltpu.make_async_copy(sent, sent, send_sem).wait()
     rest_arrived(last)
     all_stars(2 * last, finish)
     result = jnp.transpose(jnp.concatenate(pieces, axis=0))
@@ -530,9 +532,6 @@
     out[:, bodies : bodies + stars] = (
         spos + time_step * 0.5 * (svel + vel_new) + step_sq / 12.0 * (sacc - new_acc)
     )
-
-    sent = states.at[pl.ds(0, n_wide * (n_narrow + 1) - 2)]
-    pltpu.make_async_copy(sent, sent, send_sem).wait()
 
 
 def unpack(packed, gal_out, pos_out, vel_out):

time: 11.8 us -> 11.8 us (level)
  no operation moved by 1% of the time
where the time goes in v9:
time: 11.8 us; the launch traced here: 11.6 us
  Pallas kernels  11 us (93%)
  between operations  0.64 us (5%)
    pallas_call x1, Pallas kernels, body(): pl.pallas_call(functools.partial(kernel, n_wide, n_narrow), out_shape=jax...  10.4 us
    pallas_call x1, Pallas kernels, body(): pl.pallas_call(unpack, out_shape=(jax.ShapeDtypeStruct(gal_vel.shape, f32...  0.61 us

profile of v9, /device:TPU:25, one launch (start us, length us, event | category | flops | bytes accessed | tf_op | source)
XLA Modules:
  0.0 11.6 jit_solution(7716413441445375223)
XLA Ops:
  0.6 10.4 %shard_map.130.packed = f32[3,768]{1,0:T(4,128)S(1)} custom-call(f32[3,64]{1,0:T(4,128)} %star_pos_hbm.1, f32[3,64]{1,0:T(4,128)} %star_vel_hbm.1, f32[1,64]{1,0:T(1,128)} %bitcast.6, f32[3,64]{1,0:T(4,128)} %star_acc_hbm.1, f32[3,64]{1,0:T(4,128)} %star_jerk_hbm.1, f32[3,512]{1,0:T(4,128)} %gal_pos_hbm.1, f32[3,512]{1,0:T(4,128)} %gal_vel_hbm.1, ...), custom_call_target="tpu_custom_call" | custom-call | tf_op jit(solution)/shard_map/pallas_call | solution.py:564
  11.0 0.6 %shard_map.131 = (f32[3,512]{1,0:T(4,128)}, f32[3,64]{1,0:T(4,128)}, f32[3,64]{1,0:T(4,128)}) custom-call(f32[3,768]{1,0:T(4,128)S(1)} %shard_map.130.packed), custom_call_target="tpu_custom_call" | custom-call | tf_op jit(solution)/shard_map/pallas_call | solution.py:614

commit v10 on v9

--- a/solution.py
+++ b/solution.py
@@ -65,6 +65,7 @@
     out,
     star_in,
     star_mass,
+    star_rows,
     gal_in,
     masses,
     group_of,
@@ -99,15 +100,15 @@
         (star_vel_hbm, star_in.at[1], 0),
         (star_acc_hbm, star_in.at[2], 0),
         (star_jerk_hbm, star_in.at[3], 0),
-        (star_mass_hbm, star_mass, 1),
-        (gal_pos_hbm, gal_in.at[0], 2),
-        (gal_vel_hbm, gal_in.at[1], 2),
-        (gal_mass_hbm, masses.at[0], 3),
-        (group_of_hbm, group_of, 3),
-        (let_send_hbm, let_send, 4),
+        (star_mass_hbm, star_mass, 0),
+        (gal_pos_hbm, gal_in.at[0], 1),
+        (gal_vel_hbm, gal_in.at[1], 1),
+        (gal_mass_hbm, masses.at[0], 2),
+        (group_of_hbm, group_of, 2),
+        (let_send_hbm, let_send, 3),
     ]
     if kicks != n_wide:
-        fetches.append((star_leaf_hbm, star_leaf, 5))
+        fetches.append((star_leaf_hbm, star_leaf, 4))
     for source, target, i in fetches:
         pltpu.make_async_copy(source, target, in_sem.at[i]).start()
 
@@ -142,7 +143,7 @@
     row8 = lax.broadcasted_iota(jnp.int32, (ROWS, LANES), 0)
     left = lane4 < stars
 
-    fetched((star_in, 0), (star_mass, 1))
+    fetched((star_rows, 0))
     spos, svel, sacc, sjerk = (star_in[i] for i in range(4))
     pred_pos = (
         spos + time_step * svel + step_sq * 0.5 * sacc + step_sq * time_step / 6.0 * sjerk
@@ -212,9 +213,9 @@
         run(0, narrow, send_beside)
 
     def make_cells():
-        fetched((gal_in, 2), (masses, 3), (let_send, 4))
+        fetched((gal_in, 1), (masses, 2), (let_send, 3))
         if kicks != n_wide:
-            fetched((star_leaf, 5))
+            fetched((star_leaf, 4))
         gpos, gmass = gal_in[0], masses[0]
         body_lane = lax.broadcasted_iota(jnp.int32, (1, bodies), 1)
         segment = group_of[...] + (body_lane // (bodies // leaves)) * GROUPS
@@ -469,8 +470,8 @@
 
         @pl.when(second)
         def _():
+            keep(nearby(q))
             rest_arrived(q)
-            keep(nearby(q))
             all_stars(2 * q, store)
 
         @pl.when(jnp.logical_not(second))
@@ -569,12 +570,13 @@
         scratch_shapes=[
             pltpu.VMEM((4, 3, stars), f32),
             pltpu.VMEM((1, stars), f32),
+            pltpu.VMEM((13, 1, stars), f32),
             pltpu.VMEM((2, 3, bodies), f32),
             pltpu.VMEM((2, 1, bodies), f32),
             pltpu.VMEM((1, bodies), i32),
             pltpu.VMEM((1, n_wide), i32),
             pltpu.SMEM(star_leaf.shape, i32),
-            pltpu.SemaphoreType.DMA((5 + (star_leaf.shape[1] != n_wide),)),
+            pltpu.SemaphoreType.DMA((4 + (star_leaf.shape[1] != n_wide),)),
             pltpu.VMEM(((n_narrow + 1) * n_wide, 4, LANES), f32),
             pltpu.VMEM((ROWS, LANES), f32),
             pltpu.VMEM((n_wide, 4, LANES), f32),

time: 11.8 us -> 11.8 us (level)
  no operation moved by 1% of the time
where the time goes in v10:
time: 11.8 us; the launch traced here: 11.6 us
  Pallas kernels  11 us (93%)
  between operations  0.64 us (5%)
    pallas_call x1, Pallas kernels, body(): pl.pallas_call(functools.partial(kernel, n_wide, n_narrow), out_shape=jax...  10.4 us
    pallas_call x1, Pallas kernels, body(): pl.pallas_call(unpack, out_shape=(jax.ShapeDtypeStruct(gal_vel.shape, f32...  0.61 us

profile of v10, /device:TPU:25, one launch (start us, length us, event | category | flops | bytes accessed | tf_op | source)
XLA Modules:
  0.0 11.6 jit_solution(15006909410484519728)
XLA Ops:
  0.6 10.4 %shard_map.130.packed = f32[3,768]{1,0:T(4,128)S(1)} custom-call(f32[3,64]{1,0:T(4,128)} %star_pos_hbm.1, f32[3,64]{1,0:T(4,128)} %star_vel_hbm.1, f32[1,64]{1,0:T(1,128)} %bitcast.6, f32[3,64]{1,0:T(4,128)} %star_acc_hbm.1, f32[3,64]{1,0:T(4,128)} %star_jerk_hbm.1, f32[3,512]{1,0:T(4,128)} %gal_pos_hbm.1, f32[3,512]{1,0:T(4,128)} %gal_vel_hbm.1, ...), custom_call_target="tpu_custom_call" | custom-call | tf_op jit(solution)/shard_map/pallas_call | solution.py:565
  11.0 0.6 %shard_map.131 = (f32[3,512]{1,0:T(4,128)}, f32[3,64]{1,0:T(4,128)}, f32[3,64]{1,0:T(4,128)}) custom-call(f32[3,768]{1,0:T(4,128)S(1)} %shard_map.130.packed), custom_call_target="tpu_custom_call" | custom-call | tf_op jit(solution)/shard_map/pallas_call | solution.py:616
